TPU v7x, 32 devices: a whole 2x2x4 slice. The times are simulated.
32 devices in a mesh: tm: 8 (over z, x), space: 4 (over y, core).
Axes of the slice: x: 2, y: 2, z: 4, core: 2. Of those that a mesh axis runs over, the one named last changes fastest.
Arguments:
- sources: float32 [16, 4, 512, 256], P('tm', None, 'space'), may hold values from -36 to 36
- starts: float32 [16, 512, 256], P('tm', 'space'), may hold values from -24 to 24
- coupling: float32 [512], P('space'), may hold values from 0.05 to 0.25
- classes: int32 [512, 2], P('space'), may hold values from 0 to 3
- inverses: float32 [4, 128, 128], replicated, may hold values from 0 to 1
- coarse_rate: float32 [4, 128], replicated, may hold values from 0.002 to 0.5
Outputs:
- states: float32 [16, 4, 512, 256], P('tm', None, 'space')
All inputs are finite; a program needn't handle non-finite values.
Results may differ from a plain program's by a relative error of at most 0.0003.
Values sent between devices are 32-bit elements; how exact they have to be, the bound alone decides.
A program may use at most 64 MiB of HBM per device.

v0:
```python
import jax
import jax.numpy as jnp
from jax import lax
from jax.sharding import PartitionSpec as P

LB = 128
STEPS = 4


def with_halo(x, sides, width):
    for axis, dim in sides:
        count, length = (lax.axis_size(axis), x.shape[dim])
        up = [(i, (i + 1) % count) for i in range(count - 1)]
        down = [(j, i) for i, j in up]
        last = lax.slice_in_dim(x, length - width, length, axis=dim)
        first = lax.slice_in_dim(x, 0, width, axis=dim)
        before = lax.ppermute(last, axis, up)
        after = lax.ppermute(first, axis, down)
        x = jnp.concatenate([before, x, after], axis=dim)
    return x


def passed_along(block, axis, distance):
    devices = range(lax.axis_size(axis))
    route = [(i - distance, i) for i in devices if i - distance in devices]
    return lax.ppermute(block, axis, route)


def advance(field, source, coupling, classes, inverses):
    padded = with_halo(field, (("space", 1),), 1)
    rhs = field + coupling[None, :, None] * (padded[:, :-2] + padded[:, 2:]) + source
    group_count, row_count, line_len = rhs.shape
    blocked = rhs.reshape(group_count, row_count, line_len // LB, LB)
    every_class = jnp.einsum("krbj,cij->ckrbi", blocked, inverses, precision=lax.Precision.HIGHEST)
    result = every_class[0]
    for category in range(1, inverses.shape[0]):
        result = jnp.where(classes[None, :, :, None] == category, every_class[category], result)
    return result.reshape(group_count, row_count, line_len)


def shards(sources, starts, coupling, classes, inverses, coarse_rate):
    group_count = starts.shape[0]
    first_device = lax.axis_index("tm") == 0
    rates = jnp.zeros((classes.shape[0], classes.shape[1], LB), jnp.float32)
    for category in range(inverses.shape[0]):
        rates = jnp.where(
            classes[:, :, None] == category, coarse_rate[category][None, None, :], rates
        )
    decay = jnp.exp(-rates).reshape(starts.shape[1], starts.shape[2])
    fine_state = starts
    for substep in range(STEPS - 1):
        fine_state = advance(fine_state, sources[:, substep], coupling, classes, inverses)
    ends = advance(fine_state, sources[:, STEPS - 1], coupling, classes, inverses)
    incoming = passed_along(ends[-1], "tm", 1)
    entry = jnp.where(first_device, starts[0], incoming)
    fine_state = jnp.concatenate([entry[None], ends[:-1]], axis=0)
    for substep in range(STEPS - 1):
        fine_state = advance(fine_state, sources[:, substep], coupling, classes, inverses)
    resid = advance(fine_state, sources[:, STEPS - 1], coupling, classes, inverses) - ends

    def chain_from(carried):
        outputs = []
        for group in range(group_count):
            carried = decay * carried + resid[group]
            outputs.append(carried)
        return jnp.stack(outputs, axis=0)

    zeros_field = jnp.zeros_like(decay)

    def relay_turn(turn_index, carried):
        return passed_along(chain_from(carried)[-1], "tm", 1)

    entering = lax.fori_loop(0, lax.axis_size("tm") - 1, relay_turn, zeros_field)
    errors = chain_from(entering)
    finals = ends + errors
    previous = incoming + entering
    entry = jnp.where(first_device, starts[0], previous)
    fine_state = jnp.concatenate([entry[None], finals[:-1]], axis=0)
    collected = []
    for substep in range(STEPS - 1):
        fine_state = advance(fine_state, sources[:, substep], coupling, classes, inverses)
        collected.append(fine_state)
    collected.append(finals)
    return jnp.stack(collected, axis=1)


def solution(mesh):
    in_specs = (
        P("tm", None, "space", None),
        P("tm", "space", None),
        P("space"),
        P("space", None),
        P(),
        P(),
    )
    out_specs = P("tm", None, "space", None)
    return jax.shard_map(shards, mesh=mesh, in_specs=in_specs, out_specs=out_specs, check_vma=False)
```

profile of v0, /device:TPU:30, one launch (start us, length us, event | category | flops | bytes accessed | tf_op | source)
XLA Modules:
  0.0 190.3 jit_solution(9743078205226541683)
XLA Ops:
  0.9 1.9 %collective-permute-start.2 = (f32[2,1,256]{1,2,0:T(8,128)S(1)}, f32[2,1,256]{1,2,0:T(8,128)S(1)}, u32[]{:S(2)}, u32[]{:S(2)}) collective-permute-start(f32[2,1,256]{1,2,0:T(8,128)S(1)} %copy.93), channel_id=1, source_target_pairs={{1,0},{2,1},{3,2},{5,4},{6,5},{7,6},{9,8},{10,9},{11,10},{13,12},{... | collective-permute-start | bytes 6152 | tf_op jit(solution)/shard_map/ppermute | solution.py:18
  3.0 2.5 %collective-permute-start.1 = (f32[2,1,256]{1,2,0:T(8,128)S(1)}, f32[2,1,256]{1,2,0:T(8,128)S(1)}, u32[]{:S(2)}, u32[]{:S(2)}) collective-permute-start(f32[2,1,256]{1,2,0:T(8,128)S(1)} %copy.91), channel_id=1, source_target_pairs={{0,1},{1,2},{2,3},{4,5},{5,6},{6,7},{8,9},{9,10},{10,11},{12,13},{... | collective-permute-start | bytes 6152 | tf_op jit(solution)/shard_map/ppermute | solution.py:17
  5.6 1.3 fusion.97
  7.2 3.6 %collective-permute-done.1 = f32[2,1,256]{1,2,0:T(8,128)S(1)} collective-permute-done((f32[2,1,256]{1,2,0:T(8,128)S(1)}, f32[2,1,256]{1,2,0:T(8,128)S(1)}, u32[]{:S(2)}, u32[]{:S(2)}) %collective-permute-start.1) | collective-permute-done | bytes 2080 | tf_op jit(solution)/shard_map/ppermute | solution.py:17
  12.5 1.9 %collective-permute-start.4 = (f32[2,1,256]{1,2,0:T(8,128)S(1)}, f32[2,1,256]{1,2,0:T(8,128)S(1)}, u32[]{:S(2)}, u32[]{:S(2)}) collective-permute-start(f32[2,1,256]{1,2,0:T(8,128)S(1)} %get-tuple-element.155), channel_id=1, source_target_pairs={{1,0},{2,1},{3,2},{5,4},{6,5},{7,6},{9,8},{10,9},{11,10},{13,12},{... | collective-permute-start | bytes 6152 | tf_op jit(solution)/shard_map/ppermute | solution.py:18
  14.4 2.4 %collective-permute-start.3 = (f32[2,1,256]{1,2,0:T(8,128)S(1)}, f32[2,1,256]{1,2,0:T(8,128)S(1)}, u32[]{:S(2)}, u32[]{:S(2)}) collective-permute-start(f32[2,1,256]{1,2,0:T(8,128)S(1)} %get-tuple-element.154), channel_id=1, source_target_pairs={{0,1},{1,2},{2,3},{4,5},{5,6},{6,7},{8,9},{9,10},{10,11},{12,13},{... | collective-permute-start | bytes 6152 | tf_op jit(solution)/shard_map/ppermute | solution.py:17
  17.0 1.3 collective-permute-done.4
  18.3 3.8 %collective-permute-done.3 = f32[2,1,256]{1,2,0:T(8,128)S(1)} collective-permute-done((f32[2,1,256]{1,2,0:T(8,128)S(1)}, f32[2,1,256]{1,2,0:T(8,128)S(1)}, u32[]{:S(2)}, u32[]{:S(2)}) %collective-permute-start.3) | collective-permute-done | bytes 2080 | tf_op jit(solution)/shard_map/ppermute | solution.py:17
  23.7 1.9 %collective-permute-start.6 = (f32[2,1,256]{1,2,0:T(8,128)S(1)}, f32[2,1,256]{1,2,0:T(8,128)S(1)}, u32[]{:S(2)}, u32[]{:S(2)}) collective-permute-start(f32[2,1,256]{1,2,0:T(8,128)S(1)} %get-tuple-element.153), channel_id=1, source_target_pairs={{1,0},{2,1},{3,2},{5,4},{6,5},{7,6},{9,8},{10,9},{11,10},{13,12},{... | collective-permute-start | bytes 6152 | tf_op jit(solution)/shard_map/ppermute | solution.py:18
  25.6 2.4 %collective-permute-start.5 = (f32[2,1,256]{1,2,0:T(8,128)S(1)}, f32[2,1,256]{1,2,0:T(8,128)S(1)}, u32[]{:S(2)}, u32[]{:S(2)}) collective-permute-start(f32[2,1,256]{1,2,0:T(8,128)S(1)} %get-tuple-element.152), channel_id=1, source_target_pairs={{0,1},{1,2},{2,3},{4,5},{5,6},{6,7},{8,9},{9,10},{10,11},{12,13},{... | collective-permute-start | bytes 6152 | tf_op jit(solution)/shard_map/ppermute | solution.py:17
  28.2 1.3 collective-permute-done.6
  29.5 3.8 %collective-permute-done.5 = f32[2,1,256]{1,2,0:T(8,128)S(1)} collective-permute-done((f32[2,1,256]{1,2,0:T(8,128)S(1)}, f32[2,1,256]{1,2,0:T(8,128)S(1)}, u32[]{:S(2)}, u32[]{:S(2)}) %collective-permute-start.5) | collective-permute-done | bytes 2080 | tf_op jit(solution)/shard_map/ppermute | solution.py:17
  34.9 1.9 %collective-permute-start.8 = (f32[2,1,256]{1,2,0:T(8,128)S(1)}, f32[2,1,256]{1,2,0:T(8,128)S(1)}, u32[]{:S(2)}, u32[]{:S(2)}) collective-permute-start(f32[2,1,256]{1,2,0:T(8,128)S(1)} %get-tuple-element.151), channel_id=1, source_target_pairs={{1,0},{2,1},{3,2},{5,4},{6,5},{7,6},{9,8},{10,9},{11,10},{13,12},{... | collective-permute-start | bytes 6152 | tf_op jit(solution)/shard_map/ppermute | solution.py:18
  36.8 2.4 %collective-permute-start.7 = (f32[2,1,256]{1,2,0:T(8,128)S(1)}, f32[2,1,256]{1,2,0:T(8,128)S(1)}, u32[]{:S(2)}, u32[]{:S(2)}) collective-permute-start(f32[2,1,256]{1,2,0:T(8,128)S(1)} %get-tuple-element.150), channel_id=1, source_target_pairs={{0,1},{1,2},{2,3},{4,5},{5,6},{6,7},{8,9},{9,10},{10,11},{12,13},{... | collective-permute-start | bytes 6152 | tf_op jit(solution)/shard_map/ppermute | solution.py:17
  39.4 1.3 collective-permute-done.8
  40.7 3.8 %collective-permute-done.7 = f32[2,1,256]{1,2,0:T(8,128)S(1)} collective-permute-done((f32[2,1,256]{1,2,0:T(8,128)S(1)}, f32[2,1,256]{1,2,0:T(8,128)S(1)}, u32[]{:S(2)}, u32[]{:S(2)}) %collective-permute-start.7) | collective-permute-done | bytes 2080 | tf_op jit(solution)/shard_map/ppermute | solution.py:17
  45.9 1.3 collective-permute-start.9
  47.2 5.6 %collective-permute-done.9 = f32[128,256]{0,1:T(8,128)S(1)} collective-permute-done((f32[128,256]{0,1:T(8,128)S(1)}, f32[128,256]{0,1:T(8,128)S(1)}, u32[]{:S(2)}, u32[]{:S(2)}) %collective-permute-start.9) | collective-permute-done | bytes 131104 | tf_op jit(solution)/shard_map/ppermute | solution.py:26
  53.5 1.9 %collective-permute-start.11 = (f32[2,1,256]{1,2,0:T(8,128)S(1)}, f32[2,1,256]{1,2,0:T(8,128)S(1)}, u32[]{:S(2)}, u32[]{:S(2)}) collective-permute-start(f32[2,1,256]{1,2,0:T(8,128)S(1)} %get-tuple-element.147), channel_id=1, source_target_pairs={{1,0},{2,1},{3,2},{5,4},{6,5},{7,6},{9,8},{10,9},{11,10},{13,12},{... | collective-permute-start | bytes 6152 | tf_op jit(solution)/shard_map/ppermute | solution.py:18
  55.4 2.4 %collective-permute-start.10 = (f32[2,1,256]{1,2,0:T(8,128)S(1)}, f32[2,1,256]{1,2,0:T(8,128)S(1)}, u32[]{:S(2)}, u32[]{:S(2)}) collective-permute-start(f32[2,1,256]{1,2,0:T(8,128)S(1)} %get-tuple-element.146), channel_id=1, source_target_pairs={{0,1},{1,2},{2,3},{4,5},{5,6},{6,7},{8,9},{9,10},{10,11},{12,13},{... | collective-permute-start | bytes 6152 | tf_op jit(solution)/shard_map/ppermute | solution.py:17
  57.9 1.4 collective-permute-done.11
  59.3 3.8 %collective-permute-done.10 = f32[2,1,256]{1,2,0:T(8,128)S(1)} collective-permute-done((f32[2,1,256]{1,2,0:T(8,128)S(1)}, f32[2,1,256]{1,2,0:T(8,128)S(1)}, u32[]{:S(2)}, u32[]{:S(2)}) %collective-permute-start.10) | collective-permute-done | bytes 2080 | tf_op jit(solution)/shard_map/ppermute | solution.py:17
  64.7 1.9 %collective-permute-start.13 = (f32[2,1,256]{1,2,0:T(8,128)S(1)}, f32[2,1,256]{1,2,0:T(8,128)S(1)}, u32[]{:S(2)}, u32[]{:S(2)}) collective-permute-start(f32[2,1,256]{1,2,0:T(8,128)S(1)} %get-tuple-element.145), channel_id=1, source_target_pairs={{1,0},{2,1},{3,2},{5,4},{6,5},{7,6},{9,8},{10,9},{11,10},{13,12},{... | collective-permute-start | bytes 6152 | tf_op jit(solution)/shard_map/ppermute | solution.py:18
  66.7 2.4 %collective-permute-start.12 = (f32[2,1,256]{1,2,0:T(8,128)S(1)}, f32[2,1,256]{1,2,0:T(8,128)S(1)}, u32[]{:S(2)}, u32[]{:S(2)}) collective-permute-start(f32[2,1,256]{1,2,0:T(8,128)S(1)} %get-tuple-element.144), channel_id=1, source_target_pairs={{0,1},{1,2},{2,3},{4,5},{5,6},{6,7},{8,9},{9,10},{10,11},{12,13},{... | collective-permute-start | bytes 6152 | tf_op jit(solution)/shard_map/ppermute | solution.py:17
  69.1 1.4 collective-permute-done.13
  70.5 3.8 %collective-permute-done.12 = f32[2,1,256]{1,2,0:T(8,128)S(1)} collective-permute-done((f32[2,1,256]{1,2,0:T(8,128)S(1)}, f32[2,1,256]{1,2,0:T(8,128)S(1)}, u32[]{:S(2)}, u32[]{:S(2)}) %collective-permute-start.12) | collective-permute-done | bytes 2080 | tf_op jit(solution)/shard_map/ppermute | solution.py:17
  75.9 1.9 %collective-permute-start.15 = (f32[2,1,256]{1,2,0:T(8,128)S(1)}, f32[2,1,256]{1,2,0:T(8,128)S(1)}, u32[]{:S(2)}, u32[]{:S(2)}) collective-permute-start(f32[2,1,256]{1,2,0:T(8,128)S(1)} %get-tuple-element.143), channel_id=1, source_target_pairs={{1,0},{2,1},{3,2},{5,4},{6,5},{7,6},{9,8},{10,9},{11,10},{13,12},{... | collective-permute-start | bytes 6152 | tf_op jit(solution)/shard_map/ppermute | solution.py:18
  77.8 2.6 %collective-permute-start.14 = (f32[2,1,256]{1,2,0:T(8,128)S(1)}, f32[2,1,256]{1,2,0:T(8,128)S(1)}, u32[]{:S(2)}, u32[]{:S(2)}) collective-permute-start(f32[2,1,256]{1,2,0:T(8,128)S(1)} %get-tuple-element.142), channel_id=1, source_target_pairs={{0,1},{1,2},{2,3},{4,5},{5,6},{6,7},{8,9},{9,10},{10,11},{12,13},{... | collective-permute-start | bytes 6152 | tf_op jit(solution)/shard_map/ppermute | solution.py:17
  80.5 1.3 collective-permute-done.15
  81.7 3.8 %collective-permute-done.14 = f32[2,1,256]{1,2,0:T(8,128)S(1)} collective-permute-done((f32[2,1,256]{1,2,0:T(8,128)S(1)}, f32[2,1,256]{1,2,0:T(8,128)S(1)}, u32[]{:S(2)}, u32[]{:S(2)}) %collective-permute-start.14) | collective-permute-done | bytes 2080 | tf_op jit(solution)/shard_map/ppermute | solution.py:17
  87.1 1.9 %collective-permute-start.17 = (f32[2,1,256]{1,2,0:T(8,128)S(1)}, f32[2,1,256]{1,2,0:T(8,128)S(1)}, u32[]{:S(2)}, u32[]{:S(2)}) collective-permute-start(f32[2,1,256]{1,2,0:T(8,128)S(1)} %get-tuple-element.141), channel_id=1, source_target_pairs={{1,0},{2,1},{3,2},{5,4},{6,5},{7,6},{9,8},{10,9},{11,10},{13,12},{... | collective-permute-start | bytes 6152 | tf_op jit(solution)/shard_map/ppermute | solution.py:18
  89.0 2.4 %collective-permute-start.16 = (f32[2,1,256]{1,2,0:T(8,128)S(1)}, f32[2,1,256]{1,2,0:T(8,128)S(1)}, u32[]{:S(2)}, u32[]{:S(2)}) collective-permute-start(f32[2,1,256]{1,2,0:T(8,128)S(1)} %get-tuple-element.140), channel_id=1, source_target_pairs={{0,1},{1,2},{2,3},{4,5},{5,6},{6,7},{8,9},{9,10},{10,11},{12,13},{... | collective-permute-start | bytes 6152 | tf_op jit(solution)/shard_map/ppermute | solution.py:17
  91.5 1.4 collective-permute-done.17
  92.9 3.8 %collective-permute-done.16 = f32[2,1,256]{1,2,0:T(8,128)S(1)} collective-permute-done((f32[2,1,256]{1,2,0:T(8,128)S(1)}, f32[2,1,256]{1,2,0:T(8,128)S(1)}, u32[]{:S(2)}, u32[]{:S(2)}) %collective-permute-start.16) | collective-permute-done | bytes 2080 | tf_op jit(solution)/shard_map/ppermute | solution.py:17
  97.0 1.0 convolution_bitcast_fusion.3
  98.5 56.4 %while.11 = (s32[]{:T(128)}, f32[128,256]{0,1:T(8,128)S(1)}, f32[2,128,256]{1,2,0:T(8,128)S(1)}, pred[128,2]{0,1:T(4,128)(4,1)S(1)}, pred[128,2]{0,1:T(4,128)(4,...) while((s32[]{:T(128)}, f32[128,256]{0,1:T(8,128)S(1)}, ...), condition=%wide.region_1.2_spmd.clone, body=%wide.region_0.1_spmd.clone.sunk | while | flops 294914 | bytes 1053853 | solution.py:73
  98.7 1.3 collective-permute-start
  100.0 5.6 %collective-permute-done = f32[128,256]{0,1:T(8,128)S(1)} collective-permute-done((f32[128,256]{0,1:T(8,128)S(1)}, f32[128,256]{0,1:T(8,128)S(1)}, u32[]{:S(2)}, u32[]{:S(2)}) %collective-permute-start) | collective-permute-done | bytes 131104 | tf_op jit(solution)/shard_map/while/body/eval_jaxpr/ppermute | solution.py:26
  105.8 1.3 collective-permute-start
  107.1 6.0 %collective-permute-done = f32[128,256]{0,1:T(8,128)S(1)} collective-permute-done((f32[128,256]{0,1:T(8,128)S(1)}, f32[128,256]{0,1:T(8,128)S(1)}, u32[]{:S(2)}, u32[]{:S(2)}) %collective-permute-start) | collective-permute-done | bytes 131104 | tf_op jit(solution)/shard_map/while/body/eval_jaxpr/ppermute | solution.py:26
  113.3 1.3 collective-permute-start
  114.6 8.0 %collective-permute-done = f32[128,256]{0,1:T(8,128)S(1)} collective-permute-done((f32[128,256]{0,1:T(8,128)S(1)}, f32[128,256]{0,1:T(8,128)S(1)}, u32[]{:S(2)}, u32[]{:S(2)}) %collective-permute-start) | collective-permute-done | bytes 131104 | tf_op jit(solution)/shard_map/while/body/eval_jaxpr/ppermute | solution.py:26
  122.9 1.3 collective-permute-start
  124.2 7.0 %collective-permute-done = f32[128,256]{0,1:T(8,128)S(1)} collective-permute-done((f32[128,256]{0,1:T(8,128)S(1)}, f32[128,256]{0,1:T(8,128)S(1)}, u32[]{:S(2)}, u32[]{:S(2)}) %collective-permute-start) | collective-permute-done | bytes 131104 | tf_op jit(solution)/shard_map/while/body/eval_jaxpr/ppermute | solution.py:26
  131.4 1.3 collective-permute-start
  132.7 6.2 %collective-permute-done = f32[128,256]{0,1:T(8,128)S(1)} collective-permute-done((f32[128,256]{0,1:T(8,128)S(1)}, f32[128,256]{0,1:T(8,128)S(1)}, u32[]{:S(2)}, u32[]{:S(2)}) %collective-permute-start) | collective-permute-done | bytes 131104 | tf_op jit(solution)/shard_map/while/body/eval_jaxpr/ppermute | solution.py:26
  139.1 1.3 collective-permute-start
  140.4 6.5 %collective-permute-done = f32[128,256]{0,1:T(8,128)S(1)} collective-permute-done((f32[128,256]{0,1:T(8,128)S(1)}, f32[128,256]{0,1:T(8,128)S(1)}, u32[]{:S(2)}, u32[]{:S(2)}) %collective-permute-start) | collective-permute-done | bytes 131104 | tf_op jit(solution)/shard_map/while/body/eval_jaxpr/ppermute | solution.py:26
  147.1 1.3 collective-permute-start
  148.4 6.5 %collective-permute-done = f32[128,256]{0,1:T(8,128)S(1)} collective-permute-done((f32[128,256]{0,1:T(8,128)S(1)}, f32[128,256]{0,1:T(8,128)S(1)}, u32[]{:S(2)}, u32[]{:S(2)}) %collective-permute-start) | collective-permute-done | bytes 131104 | tf_op jit(solution)/shard_map/while/body/eval_jaxpr/ppermute | solution.py:26
  155.2 1.9 %collective-permute-start.19 = (f32[2,1,256]{1,2,0:T(8,128)S(1)}, f32[2,1,256]{1,2,0:T(8,128)S(1)}, u32[]{:S(2)}, u32[]{:S(2)}) collective-permute-start(f32[2,1,256]{1,2,0:T(8,128)S(1)} %get-tuple-element.139), channel_id=1, source_target_pairs={{1,0},{2,1},{3,2},{5,4},{6,5},{7,6},{9,8},{10,9},{11,10},{13,12},{... | collective-permute-start | bytes 6152 | tf_op jit(solution)/shard_map/ppermute | solution.py:18
  157.2 2.4 %collective-permute-start.18 = (f32[2,1,256]{1,2,0:T(8,128)S(1)}, f32[2,1,256]{1,2,0:T(8,128)S(1)}, u32[]{:S(2)}, u32[]{:S(2)}) collective-permute-start(f32[2,1,256]{1,2,0:T(8,128)S(1)} %get-tuple-element.138), channel_id=1, source_target_pairs={{0,1},{1,2},{2,3},{4,5},{5,6},{6,7},{8,9},{9,10},{10,11},{12,13},{... | collective-permute-start | bytes 6152 | tf_op jit(solution)/shard_map/ppermute | solution.py:17
  159.6 1.4 collective-permute-done.19
  161.0 3.8 %collective-permute-done.18 = f32[2,1,256]{1,2,0:T(8,128)S(1)} collective-permute-done((f32[2,1,256]{1,2,0:T(8,128)S(1)}, f32[2,1,256]{1,2,0:T(8,128)S(1)}, u32[]{:S(2)}, u32[]{:S(2)}) %collective-permute-start.18) | collective-permute-done | bytes 2080 | tf_op jit(solution)/shard_map/ppermute | solution.py:17
  166.5 1.9 %collective-permute-start.21 = (f32[2,1,256]{1,2,0:T(8,128)S(1)}, f32[2,1,256]{1,2,0:T(8,128)S(1)}, u32[]{:S(2)}, u32[]{:S(2)}) collective-permute-start(f32[2,1,256]{1,2,0:T(8,128)S(1)} %get-tuple-element.137), channel_id=1, source_target_pairs={{1,0},{2,1},{3,2},{5,4},{6,5},{7,6},{9,8},{10,9},{11,10},{13,12},{... | collective-permute-start | bytes 6152 | tf_op jit(solution)/shard_map/ppermute | solution.py:18
  168.4 2.4 %collective-permute-start.20 = (f32[2,1,256]{1,2,0:T(8,128)S(1)}, f32[2,1,256]{1,2,0:T(8,128)S(1)}, u32[]{:S(2)}, u32[]{:S(2)}) collective-permute-start(f32[2,1,256]{1,2,0:T(8,128)S(1)} %get-tuple-element.136), channel_id=1, source_target_pairs={{0,1},{1,2},{2,3},{4,5},{5,6},{6,7},{8,9},{9,10},{10,11},{12,13},{... | collective-permute-start | bytes 6152 | tf_op jit(solution)/shard_map/ppermute | solution.py:17
  170.8 1.4 collective-permute-done.21
  172.2 3.8 %collective-permute-done.20 = f32[2,1,256]{1,2,0:T(8,128)S(1)} collective-permute-done((f32[2,1,256]{1,2,0:T(8,128)S(1)}, f32[2,1,256]{1,2,0:T(8,128)S(1)}, u32[]{:S(2)}, u32[]{:S(2)}) %collective-permute-start.20) | collective-permute-done | bytes 2080 | tf_op jit(solution)/shard_map/ppermute | solution.py:17
  177.7 1.9 %collective-permute-start.23 = (f32[2,1,256]{1,2,0:T(8,128)S(1)}, f32[2,1,256]{1,2,0:T(8,128)S(1)}, u32[]{:S(2)}, u32[]{:S(2)}) collective-permute-start(f32[2,1,256]{1,2,0:T(8,128)S(1)} %get-tuple-element.135), channel_id=1, source_target_pairs={{1,0},{2,1},{3,2},{5,4},{6,5},{7,6},{9,8},{10,9},{11,10},{13,12},{... | collective-permute-start | bytes 6152 | tf_op jit(solution)/shard_map/ppermute | solution.py:18
  179.6 2.4 %collective-permute-start.22 = (f32[2,1,256]{1,2,0:T(8,128)S(1)}, f32[2,1,256]{1,2,0:T(8,128)S(1)}, u32[]{:S(2)}, u32[]{:S(2)}) collective-permute-start(f32[2,1,256]{1,2,0:T(8,128)S(1)} %get-tuple-element.134), channel_id=1, source_target_pairs={{0,1},{1,2},{2,3},{4,5},{5,6},{6,7},{8,9},{9,10},{10,11},{12,13},{... | collective-permute-start | bytes 6152 | tf_op jit(solution)/shard_map/ppermute | solution.py:17
  182.1 1.4 collective-permute-done.23
  183.5 3.8 %collective-permute-done.22 = f32[2,1,256]{1,2,0:T(8,128)S(1)} collective-permute-done((f32[2,1,256]{1,2,0:T(8,128)S(1)}, f32[2,1,256]{1,2,0:T(8,128)S(1)}, u32[]{:S(2)}, u32[]{:S(2)}) %collective-permute-start.22) | collective-permute-done | bytes 2080 | tf_op jit(solution)/shard_map/ppermute | solution.py:17
  187.6 1.0 convolution_bitcast_fusion
  189.0 1.3 copy.130
  (95 shorter events, 19.5 us)
Async XLA Ops:
  0.0 11.1 %copy-start = (f32[4,128,128]{2,1,0:T(8,128)S(1)}, f32[4,128,128]{2,1,0:T(8,128)}, u32[]{:S(2)}) copy-start(f32[4,128,128]{2,1,0:T(8,128)} %param.12) | copy-start | bytes 786436
  0.9 6.3 %collective-permute-start.2 = (f32[2,1,256]{1,2,0:T(8,128)S(1)}, f32[2,1,256]{1,2,0:T(8,128)S(1)}, u32[]{:S(2)}, u32[]{:S(2)}) collective-permute-start(f32[2,1,256]{1,2,0:T(8,128)S(1)} %copy.93), channel_id=1, source_target_pairs={{1,0},{2,1},{3,2},{5,4},{6,5},{7,6},{9,8},{10,9},{11,10},{13,12},{... | collective-permute-start | bytes 6152 | tf_op jit(solution)/shard_map/ppermute | solution.py:18
  3.0 3.9 %copy-start.6 = (s32[128,2]{0,1:T(2,128)S(1)}, s32[128,2]{0,1:T(2,128)}, u32[]{:S(2)}) copy-start(s32[128,2]{0,1:T(2,128)} %param.11) | copy-start | bytes 3076
  3.0 3.9 %copy-start.3 = (f32[2,128,256]{2,1,0:T(8,128)S(1)}, f32[2,128,256]{2,1,0:T(8,128)}, u32[]{:S(2)}) copy-start(f32[2,128,256]{2,1,0:T(8,128)} %param.9) | copy-start | bytes 786436
  3.0 7.8 %collective-permute-start.1 = (f32[2,1,256]{1,2,0:T(8,128)S(1)}, f32[2,1,256]{1,2,0:T(8,128)S(1)}, u32[]{:S(2)}, u32[]{:S(2)}) collective-permute-start(f32[2,1,256]{1,2,0:T(8,128)S(1)} %copy.91), channel_id=1, source_target_pairs={{0,1},{1,2},{2,3},{4,5},{5,6},{6,7},{8,9},{9,10},{10,11},{12,13},{... | collective-permute-start | bytes 6152 | tf_op jit(solution)/shard_map/ppermute | solution.py:17
  7.1 3.8 %copy-start.4 = (f32[128]{0:T(128)S(1)}, f32[128]{0:T(128)}, u32[]{:S(2)}) copy-start(f32[128]{0:T(128)} %param.10) | copy-start | bytes 1540
  12.5 5.8 %collective-permute-start.4 = (f32[2,1,256]{1,2,0:T(8,128)S(1)}, f32[2,1,256]{1,2,0:T(8,128)S(1)}, u32[]{:S(2)}, u32[]{:S(2)}) collective-permute-start(f32[2,1,256]{1,2,0:T(8,128)S(1)} %get-tuple-element.155), channel_id=1, source_target_pairs={{1,0},{2,1},{3,2},{5,4},{6,5},{7,6},{9,8},{10,9},{11,10},{13,12},{... | collective-permute-start | bytes 6152 | tf_op jit(solution)/shard_map/ppermute | solution.py:18
  14.4 7.7 %collective-permute-start.3 = (f32[2,1,256]{1,2,0:T(8,128)S(1)}, f32[2,1,256]{1,2,0:T(8,128)S(1)}, u32[]{:S(2)}, u32[]{:S(2)}) collective-permute-start(f32[2,1,256]{1,2,0:T(8,128)S(1)} %get-tuple-element.154), channel_id=1, source_target_pairs={{0,1},{1,2},{2,3},{4,5},{5,6},{6,7},{8,9},{9,10},{10,11},{12,13},{... | collective-permute-start | bytes 6152 | tf_op jit(solution)/shard_map/ppermute | solution.py:17
  23.7 5.8 %collective-permute-start.6 = (f32[2,1,256]{1,2,0:T(8,128)S(1)}, f32[2,1,256]{1,2,0:T(8,128)S(1)}, u32[]{:S(2)}, u32[]{:S(2)}) collective-permute-start(f32[2,1,256]{1,2,0:T(8,128)S(1)} %get-tuple-element.153), channel_id=1, source_target_pairs={{1,0},{2,1},{3,2},{5,4},{6,5},{7,6},{9,8},{10,9},{11,10},{13,12},{... | collective-permute-start | bytes 6152 | tf_op jit(solution)/shard_map/ppermute | solution.py:18
  25.6 7.7 %collective-permute-start.5 = (f32[2,1,256]{1,2,0:T(8,128)S(1)}, f32[2,1,256]{1,2,0:T(8,128)S(1)}, u32[]{:S(2)}, u32[]{:S(2)}) collective-permute-start(f32[2,1,256]{1,2,0:T(8,128)S(1)} %get-tuple-element.152), channel_id=1, source_target_pairs={{0,1},{1,2},{2,3},{4,5},{5,6},{6,7},{8,9},{9,10},{10,11},{12,13},{... | collective-permute-start | bytes 6152 | tf_op jit(solution)/shard_map/ppermute | solution.py:17
  34.9 5.8 %collective-permute-start.8 = (f32[2,1,256]{1,2,0:T(8,128)S(1)}, f32[2,1,256]{1,2,0:T(8,128)S(1)}, u32[]{:S(2)}, u32[]{:S(2)}) collective-permute-start(f32[2,1,256]{1,2,0:T(8,128)S(1)} %get-tuple-element.151), channel_id=1, source_target_pairs={{1,0},{2,1},{3,2},{5,4},{6,5},{7,6},{9,8},{10,9},{11,10},{13,12},{... | collective-permute-start | bytes 6152 | tf_op jit(solution)/shard_map/ppermute | solution.py:18
  36.8 7.7 %collective-permute-start.7 = (f32[2,1,256]{1,2,0:T(8,128)S(1)}, f32[2,1,256]{1,2,0:T(8,128)S(1)}, u32[]{:S(2)}, u32[]{:S(2)}) collective-permute-start(f32[2,1,256]{1,2,0:T(8,128)S(1)} %get-tuple-element.150), channel_id=1, source_target_pairs={{0,1},{1,2},{2,3},{4,5},{5,6},{6,7},{8,9},{9,10},{10,11},{12,13},{... | collective-permute-start | bytes 6152 | tf_op jit(solution)/shard_map/ppermute | solution.py:17
  45.9 6.9 %collective-permute-start.9 = (f32[128,256]{0,1:T(8,128)S(1)}, f32[128,256]{0,1:T(8,128)S(1)}, u32[]{:S(2)}, u32[]{:S(2)}) collective-permute-start(f32[128,256]{0,1:T(8,128)S(1)} %bitcast.480), channel_id=1, source_target_pairs={{0,4},{4,8},{8,12},{12,16},{16,20},{20,24},{24,28},{1,5},{5,9},{9,... | collective-permute-start | bytes 393224 | tf_op jit(solution)/shard_map/ppermute | solution.py:26
  52.7 0.7 copy-start.1
  53.5 5.8 %collective-permute-start.11 = (f32[2,1,256]{1,2,0:T(8,128)S(1)}, f32[2,1,256]{1,2,0:T(8,128)S(1)}, u32[]{:S(2)}, u32[]{:S(2)}) collective-permute-start(f32[2,1,256]{1,2,0:T(8,128)S(1)} %get-tuple-element.147), channel_id=1, source_target_pairs={{1,0},{2,1},{3,2},{5,4},{6,5},{7,6},{9,8},{10,9},{11,10},{13,12},{... | collective-permute-start | bytes 6152 | tf_op jit(solution)/shard_map/ppermute | solution.py:18
  55.4 7.7 %collective-permute-start.10 = (f32[2,1,256]{1,2,0:T(8,128)S(1)}, f32[2,1,256]{1,2,0:T(8,128)S(1)}, u32[]{:S(2)}, u32[]{:S(2)}) collective-permute-start(f32[2,1,256]{1,2,0:T(8,128)S(1)} %get-tuple-element.146), channel_id=1, source_target_pairs={{0,1},{1,2},{2,3},{4,5},{5,6},{6,7},{8,9},{9,10},{10,11},{12,13},{... | collective-permute-start | bytes 6152 | tf_op jit(solution)/shard_map/ppermute | solution.py:17
  64.7 4.4 %copy-start.5 = (f32[4,128]{1,0:T(4,128)S(1)}, f32[4,128]{1,0:T(4,128)}, u32[]{:S(2)}) copy-start(f32[4,128]{1,0:T(4,128)} %param.13) | copy-start | bytes 6148
  64.7 5.8 %collective-permute-start.13 = (f32[2,1,256]{1,2,0:T(8,128)S(1)}, f32[2,1,256]{1,2,0:T(8,128)S(1)}, u32[]{:S(2)}, u32[]{:S(2)}) collective-permute-start(f32[2,1,256]{1,2,0:T(8,128)S(1)} %get-tuple-element.145), channel_id=1, source_target_pairs={{1,0},{2,1},{3,2},{5,4},{6,5},{7,6},{9,8},{10,9},{11,10},{13,12},{... | collective-permute-start | bytes 6152 | tf_op jit(solution)/shard_map/ppermute | solution.py:18
  66.7 7.7 %collective-permute-start.12 = (f32[2,1,256]{1,2,0:T(8,128)S(1)}, f32[2,1,256]{1,2,0:T(8,128)S(1)}, u32[]{:S(2)}, u32[]{:S(2)}) collective-permute-start(f32[2,1,256]{1,2,0:T(8,128)S(1)} %get-tuple-element.144), channel_id=1, source_target_pairs={{0,1},{1,2},{2,3},{4,5},{5,6},{6,7},{8,9},{9,10},{10,11},{12,13},{... | collective-permute-start | bytes 6152 | tf_op jit(solution)/shard_map/ppermute | solution.py:17
  75.9 5.8 %collective-permute-start.15 = (f32[2,1,256]{1,2,0:T(8,128)S(1)}, f32[2,1,256]{1,2,0:T(8,128)S(1)}, u32[]{:S(2)}, u32[]{:S(2)}) collective-permute-start(f32[2,1,256]{1,2,0:T(8,128)S(1)} %get-tuple-element.143), channel_id=1, source_target_pairs={{1,0},{2,1},{3,2},{5,4},{6,5},{7,6},{9,8},{10,9},{11,10},{13,12},{... | collective-permute-start | bytes 6152 | tf_op jit(solution)/shard_map/ppermute | solution.py:18
  77.8 7.7 %collective-permute-start.14 = (f32[2,1,256]{1,2,0:T(8,128)S(1)}, f32[2,1,256]{1,2,0:T(8,128)S(1)}, u32[]{:S(2)}, u32[]{:S(2)}) collective-permute-start(f32[2,1,256]{1,2,0:T(8,128)S(1)} %get-tuple-element.142), channel_id=1, source_target_pairs={{0,1},{1,2},{2,3},{4,5},{5,6},{6,7},{8,9},{9,10},{10,11},{12,13},{... | collective-permute-start | bytes 6152 | tf_op jit(solution)/shard_map/ppermute | solution.py:17
  87.1 5.8 %collective-permute-start.17 = (f32[2,1,256]{1,2,0:T(8,128)S(1)}, f32[2,1,256]{1,2,0:T(8,128)S(1)}, u32[]{:S(2)}, u32[]{:S(2)}) collective-permute-start(f32[2,1,256]{1,2,0:T(8,128)S(1)} %get-tuple-element.141), channel_id=1, source_target_pairs={{1,0},{2,1},{3,2},{5,4},{6,5},{7,6},{9,8},{10,9},{11,10},{13,12},{... | collective-permute-start | bytes 6152 | tf_op jit(solution)/shard_map/ppermute | solution.py:18
  89.0 7.7 %collective-permute-start.16 = (f32[2,1,256]{1,2,0:T(8,128)S(1)}, f32[2,1,256]{1,2,0:T(8,128)S(1)}, u32[]{:S(2)}, u32[]{:S(2)}) collective-permute-start(f32[2,1,256]{1,2,0:T(8,128)S(1)} %get-tuple-element.140), channel_id=1, source_target_pairs={{0,1},{1,2},{2,3},{4,5},{5,6},{6,7},{8,9},{9,10},{10,11},{12,13},{... | collective-permute-start | bytes 6152 | tf_op jit(solution)/shard_map/ppermute | solution.py:17
  98.4 56.4 %copy-start.2 = (f32[128,256]{0,1:T(8,128)S(1)}, f32[128,256]{0,1:T(8,128)}, u32[]{:S(2)}) copy-start(f32[128,256]{0,1:T(8,128)} %copy-done.1) | copy-start | bytes 393220
  98.7 6.9 %collective-permute-start = (f32[128,256]{0,1:T(8,128)S(1)}, f32[128,256]{0,1:T(8,128)S(1)}, u32[]{:S(2)}, u32[]{:S(2)}) collective-permute-start(f32[128,256]{0,1:T(8,128)S(1)} %bitcast_add_fusion.3), channel_id=1, source_target_pairs={{0,4},{4,8},{8,12},{12,16},{16,20},{20,24},{24,28},{1,5},{5,9},{9,... | collective-permute-start | bytes 393224 | tf_op jit(solution)/shard_map/while/body/eval_jaxpr/ppermute | solution.py:26
  105.8 7.3 %collective-permute-start = (f32[128,256]{0,1:T(8,128)S(1)}, f32[128,256]{0,1:T(8,128)S(1)}, u32[]{:S(2)}, u32[]{:S(2)}) collective-permute-start(f32[128,256]{0,1:T(8,128)S(1)} %bitcast_add_fusion.3), channel_id=1, source_target_pairs={{0,4},{4,8},{8,12},{12,16},{16,20},{20,24},{24,28},{1,5},{5,9},{9,... | collective-permute-start | bytes 393224 | tf_op jit(solution)/shard_map/while/body/eval_jaxpr/ppermute | solution.py:26
  113.3 9.4 %collective-permute-start = (f32[128,256]{0,1:T(8,128)S(1)}, f32[128,256]{0,1:T(8,128)S(1)}, u32[]{:S(2)}, u32[]{:S(2)}) collective-permute-start(f32[128,256]{0,1:T(8,128)S(1)} %bitcast_add_fusion.3), channel_id=1, source_target_pairs={{0,4},{4,8},{8,12},{12,16},{16,20},{20,24},{24,28},{1,5},{5,9},{9,... | collective-permute-start | bytes 393224 | tf_op jit(solution)/shard_map/while/body/eval_jaxpr/ppermute | solution.py:26
  122.9 8.3 %collective-permute-start = (f32[128,256]{0,1:T(8,128)S(1)}, f32[128,256]{0,1:T(8,128)S(1)}, u32[]{:S(2)}, u32[]{:S(2)}) collective-permute-start(f32[128,256]{0,1:T(8,128)S(1)} %bitcast_add_fusion.3), channel_id=1, source_target_pairs={{0,4},{4,8},{8,12},{12,16},{16,20},{20,24},{24,28},{1,5},{5,9},{9,... | collective-permute-start | bytes 393224 | tf_op jit(solution)/shard_map/while/body/eval_jaxpr/ppermute | solution.py:26
  131.4 7.5 %collective-permute-start = (f32[128,256]{0,1:T(8,128)S(1)}, f32[128,256]{0,1:T(8,128)S(1)}, u32[]{:S(2)}, u32[]{:S(2)}) collective-permute-start(f32[128,256]{0,1:T(8,128)S(1)} %bitcast_add_fusion.3), channel_id=1, source_target_pairs={{0,4},{4,8},{8,12},{12,16},{16,20},{20,24},{24,28},{1,5},{5,9},{9,... | collective-permute-start | bytes 393224 | tf_op jit(solution)/shard_map/while/body/eval_jaxpr/ppermute | solution.py:26
  139.1 7.8 %collective-permute-start = (f32[128,256]{0,1:T(8,128)S(1)}, f32[128,256]{0,1:T(8,128)S(1)}, u32[]{:S(2)}, u32[]{:S(2)}) collective-permute-start(f32[128,256]{0,1:T(8,128)S(1)} %bitcast_add_fusion.3), channel_id=1, source_target_pairs={{0,4},{4,8},{8,12},{12,16},{16,20},{20,24},{24,28},{1,5},{5,9},{9,... | collective-permute-start | bytes 393224 | tf_op jit(solution)/shard_map/while/body/eval_jaxpr/ppermute | solution.py:26
  147.1 7.8 %collective-permute-start = (f32[128,256]{0,1:T(8,128)S(1)}, f32[128,256]{0,1:T(8,128)S(1)}, u32[]{:S(2)}, u32[]{:S(2)}) collective-permute-start(f32[128,256]{0,1:T(8,128)S(1)} %bitcast_add_fusion.3), channel_id=1, source_target_pairs={{0,4},{4,8},{8,12},{12,16},{16,20},{20,24},{24,28},{1,5},{5,9},{9,... | collective-permute-start | bytes 393224 | tf_op jit(solution)/shard_map/while/body/eval_jaxpr/ppermute | solution.py:26
  155.2 5.8 %collective-permute-start.19 = (f32[2,1,256]{1,2,0:T(8,128)S(1)}, f32[2,1,256]{1,2,0:T(8,128)S(1)}, u32[]{:S(2)}, u32[]{:S(2)}) collective-permute-start(f32[2,1,256]{1,2,0:T(8,128)S(1)} %get-tuple-element.139), channel_id=1, source_target_pairs={{1,0},{2,1},{3,2},{5,4},{6,5},{7,6},{9,8},{10,9},{11,10},{13,12},{... | collective-permute-start | bytes 6152 | tf_op jit(solution)/shard_map/ppermute | solution.py:18
  157.2 7.7 %collective-permute-start.18 = (f32[2,1,256]{1,2,0:T(8,128)S(1)}, f32[2,1,256]{1,2,0:T(8,128)S(1)}, u32[]{:S(2)}, u32[]{:S(2)}) collective-permute-start(f32[2,1,256]{1,2,0:T(8,128)S(1)} %get-tuple-element.138), channel_id=1, source_target_pairs={{0,1},{1,2},{2,3},{4,5},{5,6},{6,7},{8,9},{9,10},{10,11},{12,13},{... | collective-permute-start | bytes 6152 | tf_op jit(solution)/shard_map/ppermute | solution.py:17
  166.5 5.8 %collective-permute-start.21 = (f32[2,1,256]{1,2,0:T(8,128)S(1)}, f32[2,1,256]{1,2,0:T(8,128)S(1)}, u32[]{:S(2)}, u32[]{:S(2)}) collective-permute-start(f32[2,1,256]{1,2,0:T(8,128)S(1)} %get-tuple-element.137), channel_id=1, source_target_pairs={{1,0},{2,1},{3,2},{5,4},{6,5},{7,6},{9,8},{10,9},{11,10},{13,12},{... | collective-permute-start | bytes 6152 | tf_op jit(solution)/shard_map/ppermute | solution.py:18
  168.4 7.7 %collective-permute-start.20 = (f32[2,1,256]{1,2,0:T(8,128)S(1)}, f32[2,1,256]{1,2,0:T(8,128)S(1)}, u32[]{:S(2)}, u32[]{:S(2)}) collective-permute-start(f32[2,1,256]{1,2,0:T(8,128)S(1)} %get-tuple-element.136), channel_id=1, source_target_pairs={{0,1},{1,2},{2,3},{4,5},{5,6},{6,7},{8,9},{9,10},{10,11},{12,13},{... | collective-permute-start | bytes 6152 | tf_op jit(solution)/shard_map/ppermute | solution.py:17
  177.7 5.8 %collective-permute-start.23 = (f32[2,1,256]{1,2,0:T(8,128)S(1)}, f32[2,1,256]{1,2,0:T(8,128)S(1)}, u32[]{:S(2)}, u32[]{:S(2)}) collective-permute-start(f32[2,1,256]{1,2,0:T(8,128)S(1)} %get-tuple-element.135), channel_id=1, source_target_pairs={{1,0},{2,1},{3,2},{5,4},{6,5},{7,6},{9,8},{10,9},{11,10},{13,12},{... | collective-permute-start | bytes 6152 | tf_op jit(solution)/shard_map/ppermute | solution.py:18
  179.6 7.7 %collective-permute-start.22 = (f32[2,1,256]{1,2,0:T(8,128)S(1)}, f32[2,1,256]{1,2,0:T(8,128)S(1)}, u32[]{:S(2)}, u32[]{:S(2)}) collective-permute-start(f32[2,1,256]{1,2,0:T(8,128)S(1)} %get-tuple-element.134), channel_id=1, source_target_pairs={{0,1},{1,2},{2,3},{4,5},{5,6},{6,7},{8,9},{9,10},{10,11},{12,13},{... | collective-permute-start | bytes 6152 | tf_op jit(solution)/shard_map/ppermute | solution.py:17
where the time goes:
time: 194 us; the launch traced here: 190 us
  waiting for transfers between devices  107 us (55%)
  starting transfers between devices  58.4 us (30%)
  matrix products  11 us (6%)
  local copies, waits for them, and re-layouts  7.04 us (4%)
  other arithmetic  6.1 us (3%)
    ppermute x8, waiting for transfers between devices, passed_along(): return lax.ppermute(block, axis, route)  51.3 us
    ppermute x11, waiting for transfers between devices, with_halo(): before = lax.ppermute(last, axis, up)  41.9 us
    ppermute x11, starting transfers between devices, with_halo(): before = lax.ppermute(last, axis, up)  26.9 us
    ppermute x11, starting transfers between devices, with_halo(): after = lax.ppermute(first, axis, down)  21.1 us
    ppermute x11, waiting for transfers between devices, with_halo(): after = lax.ppermute(first, axis, down)  13.7 us
    dot_general x11, matrix products, advance(): jnp.einsum('krbj,cij->ckrbi', blocked, inverses, precision=lax.Precision....  11 us
    ppermute x8, starting transfers between devices, passed_along(): return lax.ppermute(block, axis, route)  10.3 us
  transfers between devices with their start and end apart: 30, of which 29 were waited for; matrix products, arithmetic and copies ran while one was open for 1% of the time, Pallas kernels for 0%

commit v1 on v0

v1 whole, which is shorter than its diff:
```python
import functools

import jax
import jax.numpy as jnp
from jax import lax
from jax.experimental import pallas as pl
from jax.experimental.pallas import tpu as pltpu
from jax.sharding import PartitionSpec as P

PAD = 8
CHUNKS = 3
VMEM_LIMIT = 60 * 1024 * 1024
MESH = pl.DeviceIdType.MESH


def ceil8(x):
    return -(-x // 8) * 8


def kernel(cfg, sources, starts, coupling, classes, inverses, rate, out,
           F, S, CPH, CLH, CP, MK, OD, W, FIN, ENDS, RES, DEC, R, RP, EI, EP, EN, FW, DL, OB,
           in_sem, hs, hr, es, er, rs, rr, fs, fr, ps, pr, out_sem):
    tm, space = cfg
    G, RL, L = starts.shape
    steps = sources.shape[1]
    C, LB, _ = inverses.shape
    B = L // LB
    KH = C // 2
    T = 3 * steps - 1
    HM = ceil8(T)
    HB = ceil8(T - steps)
    NB = RL + 2 * HB
    HALF = NB // 2
    CH = HALF // CHUNKS
    f32, bf16 = jnp.float32, jnp.bfloat16
    t = lax.axis_index("tm")
    s = lax.axis_index("space")
    p = lax.rem(t, 2)
    partner = t + 1 - 2 * p
    has_up, has_dn = s > 0, s < space - 1
    has_prev, has_next = t > 0, t < tm - 1
    has_pz, has_nz = t > 1, t < tm - 2

    own = pl.ds(HM, RL)
    in_starts = pltpu.make_async_copy(starts, F.at[:, pl.ds(PAD + HM, RL), :], in_sem.at[0])
    in_starts.start()
    in_src = [
        pltpu.make_async_copy(sources.at[:, m], S.at[:, m, own, :], in_sem.at[1 + m])
        for m in range(steps)
    ]
    for c in in_src:
        c.start()

    barrier = pltpu.get_barrier_semaphore()
    peers = [
        (has_up, (t, s - 1)), (has_dn, (t, s + 1)),
        (has_prev, (t - 1, s)), (has_next, (t + 1, s)),
        (has_pz, (t - 2, s)), (has_nz, (t + 2, s)),
    ]
    for cond, dev in peers:
        @pl.when(cond)
        def _(dev=dev):
            pl.semaphore_signal(barrier, inc=1, device_id=dev, device_id_type=MESH)
    pl.semaphore_wait(barrier, sum(jnp.where(cond, 1, 0) for cond, _ in peers))

    def remote(src, dst, a, b, dev):
        return pltpu.make_async_remote_copy(
            src_ref=src, dst_ref=dst, send_sem=a, recv_sem=b, device_id=dev, device_id_type=MESH
        )

    down, up = [], []
    halves = [HM if T - (m + 1) > HM - 8 else ceil8(T - (m + 1)) for m in range(steps)]
    down.append((coupling, CPH.at[0]))
    up.append((coupling, CPH.at[1]))
    down.append((classes, CLH.at[0]))
    up.append((classes, CLH.at[1]))
    down.append((starts.at[:, pl.ds(RL - HM, HM), :], F.at[:, pl.ds(PAD, HM), :]))
    up.append((starts.at[:, pl.ds(0, HM), :], F.at[:, pl.ds(PAD + HM + RL, HM), :]))
    for m in range(steps):
        h = halves[m]
        down.append((sources.at[:, m, pl.ds(RL - h, h), :], S.at[:, m, pl.ds(HM - h, h), :]))
        up.append((sources.at[:, m, pl.ds(0, h), :], S.at[:, m, pl.ds(HM + RL, h), :]))
    n_halo = len(down)
    down = [remote(a, b, hs.at[0, i], hr.at[0, i], (t, s + 1)) for i, (a, b) in enumerate(down)]
    up = [remote(a, b, hs.at[1, i], hr.at[1, i], (t, s - 1)) for i, (a, b) in enumerate(up)]

    @pl.when(has_dn)
    def _():
        for c in down:
            c.start()

    @pl.when(has_up)
    def _():
        for c in up:
            c.start()

    def clear(side):
        CPH[side] = jnp.zeros(CPH.shape[1:], f32)
        CLH[side] = jnp.zeros(CLH.shape[1:], jnp.int32)
        F[:, pl.ds(PAD + side * (HM + RL), HM), :] = jnp.zeros((G, HM, L), f32)
        S[:, :, pl.ds(side * (HM + RL), HM), :] = jnp.zeros((G, steps, HM, L), f32)

    @pl.when(jnp.logical_not(has_up))
    def _():
        clear(0)

    @pl.when(jnp.logical_not(has_dn))
    def _():
        clear(1)

    for g in range(G):
        F[g, pl.ds(0, PAD), :] = jnp.zeros((PAD, L), f32)
        F[g, pl.ds(PAD + HM * 2 + RL, PAD), :] = jnp.zeros((PAD, L), f32)

    for k in range(KH):
        for o in range(2):
            wt = inverses[2 * k + o].T
            hi = wt.astype(bf16)
            lo = (wt - hi.astype(f32)).astype(bf16)
            cols = pl.ds(o * LB, LB)
            W[pl.ds(k * LB, LB), cols] = hi
            W[pl.ds((KH + k) * LB, LB), cols] = hi
            W[pl.ds((2 * KH + k) * LB, LB), cols] = lo

    def column(row):
        return jnp.broadcast_to(row, (LB, RL)).T

    def fields(row, cls, part, n):
        for b in range(B):
            cl = column(cls[b : b + 1, :].astype(f32))[part]
            for k in range(KH):
                MK[b, k, pl.ds(row, n), :] = jnp.where((cl == 2 * k) | (cl == 2 * k + 1), 1.0, 0.0).astype(bf16)
            odd = cl == 1
            for k in range(1, KH):
                odd = odd | (cl == 2 * k + 1)
            OD[b, pl.ds(row, n), :] = jnp.where(odd, 1.0, 0.0)
            r = jnp.broadcast_to(rate[0:1, :], (n, LB))
            for c in range(1, C):
                r = jnp.where(cl == c, jnp.broadcast_to(rate[c : c + 1, :], (n, LB)), r)
            DEC[pl.ds(row, n), pl.ds(b * LB, LB)] = jnp.exp(-r)

    CP[own, :] = column(coupling[...])
    fields(HM, classes[...], slice(0, RL), RL)

    @pl.when(has_up)
    def _():
        for c in down:
            c.wait_recv()

    @pl.when(has_dn)
    def _():
        for c in up:
            c.wait_recv()

    CP[pl.ds(0, HM), :] = column(CPH[0])[RL - HM :]
    CP[pl.ds(HM + RL, HM), :] = column(CPH[1])[:HM]
    fields(0, CLH[0], slice(RL - HM, RL), HM)
    fields(HM + RL, CLH[1], slice(0, HM), HM)

    in_starts.wait()
    for c in in_src:
        c.wait()

    big = pl.ds(HM - HB, NB)
    fbig = pl.ds(PAD + HM - HB, NB)

    @pl.when(jnp.logical_not(has_prev))
    def _():
        FIN[...] = F[0, fbig, :]

    def phi(g, m, t_step):
        h = ceil8(T - t_step)
        lo, n = HM - h, RL + 2 * h
        xs = []
        for b in range(B):
            ln = pl.ds(b * LB, LB)
            v = F[g, pl.ds(PAD + lo, n), ln]
            a = F[g, pl.ds(PAD + lo - 1, n), ln]
            d = F[g, pl.ds(PAD + lo + 1, n), ln]
            rhs = v + CP[pl.ds(lo, n), :] * (a + d) + S[g, m, pl.ds(lo, n), ln]
            hi = rhs.astype(bf16)
            low = (rhs - hi.astype(f32)).astype(bf16)
            mk = [MK[b, k, pl.ds(lo, n), :] for k in range(KH)]
            his = [hi * q for q in mk]
            xs.append(jnp.concatenate(his + [low * q for q in mk] + his, axis=1))
        y = jnp.dot(jnp.concatenate(xs, axis=0), W[...], preferred_element_type=f32)
        res = []
        for b in range(B):
            odd = OD[b, pl.ds(lo, n), :] > 0.5
            yb = y[b * n : (b + 1) * n]
            res.append(jnp.where(odd, yb[:, LB:], yb[:, :LB]))
        return jnp.concatenate(res, axis=1), lo, n

    def relax(g, first):
        for m in range(steps - 1):
            res, lo, n = phi(g, m, first + m)
            F[g, pl.ds(PAD + lo, n), :] = res

    send_ends = remote(ENDS.at[G - 1], FIN, es.at[0], er.at[0], (t + 1, s))
    for g in [G - 1] + list(range(G - 1)):
        relax(g, 1)
        res, lo, n = phi(g, steps - 1, steps)
        ENDS[g] = res
        if g == G - 1:
            @pl.when(has_next)
            def _():
                send_ends.start()

    for g in list(range(1, G)) + [0]:
        if g == 0:
            @pl.when(has_prev)
            def _():
                send_ends.wait_recv()
            F[g, fbig, :] = FIN[...]
        else:
            F[g, fbig, :] = ENDS[g - 1]
        relax(g, steps + 1)
        res, lo, n = phi(g, steps - 1, 2 * steps)
        RES[g] = res - ENDS[g]

    dec = DEC[big, :]
    acc = RES[0]
    for g in range(1, G):
        acc = dec * acc + RES[g]
    R[...] = acc
    keep = pl.multiple_of((1 - p) * HALF, 8)
    give = pl.multiple_of(p * HALF, 8)
    swap = remote(R.at[pl.ds(give, HALF), :], RP, rs.at[0], rr.at[0], (partner, s))
    swap.start()

    @pl.when(jnp.logical_not(has_pz))
    def _():
        EI[...] = jnp.zeros((HALF, L), f32)

    chunk = [pl.ds(j * CH, CH) for j in range(CHUNKS)]
    forward = [remote(FW.at[c], EI.at[c], fs.at[j], fr.at[j], (t + 2, s)) for j, c in enumerate(chunk)]
    deliver0 = [remote(DL.at[c], EP.at[c], ps.at[j], pr.at[j], (partner, s)) for j, c in enumerate(chunk)]
    deliver1 = [remote(EI.at[c], EP.at[c], ps.at[j], pr.at[j], (partner, s)) for j, c in enumerate(chunk)]
    swap.wait_recv()
    for j in range(CHUNKS):
        mine = pl.ds(pl.multiple_of(keep + j * CH, 8), CH)
        c = chunk[j]
        d1 = DEC[pl.ds(pl.multiple_of(HM - HB + keep + j * CH, 8), CH), :]
        D = d1
        for _ in range(1, G):
            D = D * d1
        r_own, r_other = R[mine, :], RP[c, :]
        first = jnp.where(p == 0, r_own, r_other)
        second = jnp.where(p == 0, r_other, r_own)

        @pl.when(has_pz)
        def _():
            forward[j].wait_recv()

        mid = D * EI[c, :] + first

        @pl.when(has_nz)
        def _():
            FW[c, :] = D * mid + second
            forward[j].start()

        @pl.when(p == 0)
        def _():
            DL[c, :] = mid
            deliver0[j].start()
            EN[mine, :] = EI[c, :]

        @pl.when(p == 1)
        def _():
            deliver1[j].start()
            EN[mine, :] = mid

    for j in range(CHUNKS):
        deliver0[j].wait_recv()
    EN[pl.ds(give, HALF), :] = EP[...]

    e = EN[...]
    outs = []
    F[0, fbig, :] = FIN[...] + e
    for g in range(G):
        e = dec * e + RES[g]
        fin = ENDS[g] + e
        OB[g, steps - 1] = fin[HB : HB + RL]
        if g + 1 < G:
            F[g + 1, fbig, :] = fin
    for g in range(G):
        c = pltpu.make_async_copy(OB.at[g, steps - 1], out.at[g, steps - 1], out_sem.at[g, steps - 1])
        c.start()
        outs.append(c)
    for m in range(steps - 1):
        for g in range(G):
            res, lo, n = phi(g, m, 2 * steps + 1 + m)
            if m < steps - 2:
                F[g, pl.ds(PAD + lo, n), :] = res
            OB[g, m] = res[HM - lo : HM - lo + RL]
            c = pltpu.make_async_copy(OB.at[g, m], out.at[g, m], out_sem.at[g, m])
            c.start()
            outs.append(c)
    for c in outs:
        c.wait()

    @pl.when(has_dn)
    def _():
        for c in down:
            c.wait_send()

    @pl.when(has_up)
    def _():
        for c in up:
            c.wait_send()

    @pl.when(has_next)
    def _():
        send_ends.wait_send()

    swap.wait_send()

    @pl.when(has_nz)
    def _():
        for c in forward:
            c.wait_send()

    for c in deliver0:
        c.wait_send()


def shards(cfg, sources, starts, coupling, classes, inverses, coarse_rate):
    G, RL, L = starts.shape
    steps = sources.shape[1]
    C, LB, _ = inverses.shape
    B = L // LB
    T = 3 * steps - 1
    HM = ceil8(T)
    NB = RL + 2 * ceil8(T - steps)
    HALF = NB // 2
    E = RL + 2 * HM
    f32, bf16 = jnp.float32, jnp.bfloat16
    dma = pltpu.SemaphoreType.DMA
    vm = pltpu.VMEM
    n_halo = 3 + steps
    return pl.pallas_call(
        functools.partial(kernel, cfg),
        out_shape=jax.ShapeDtypeStruct(sources.shape, f32),
        in_specs=[pl.BlockSpec(memory_space=pl.ANY)] * 2 + [pl.BlockSpec(memory_space=pltpu.VMEM)] * 4,
        out_specs=pl.BlockSpec(memory_space=pl.ANY),
        scratch_shapes=[
            vm((G, E + 2 * PAD, L), f32),
            vm((G, steps, E, L), f32),
            vm((2, 1, RL), f32),
            vm((2, B, RL), jnp.int32),
            vm((E, LB), f32),
            vm((B, C // 2, E, LB), bf16),
            vm((B, E, LB), f32),
            vm((3 * C // 2 * LB, 2 * LB), bf16),
            vm((NB, L), f32),
            vm((G, NB, L), f32),
            vm((G, NB, L), f32),
            vm((E, L), f32),
            vm((NB, L), f32),
            vm((HALF, L), f32),
            vm((HALF, L), f32),
            vm((HALF, L), f32),
            vm((NB, L), f32),
            vm((HALF, L), f32),
            vm((HALF, L), f32),
            vm((G, steps, RL, L), f32),
            dma((1 + steps,)),
            dma((2, n_halo)), dma((2, n_halo)),
            dma((1,)), dma((1,)),
            dma((1,)), dma((1,)),
            dma((CHUNKS,)), dma((CHUNKS,)),
            dma((CHUNKS,)), dma((CHUNKS,)),
            dma((G, steps)),
        ],
        compiler_params=pltpu.CompilerParams(
            collective_id=0, has_side_effects=True, vmem_limit_bytes=VMEM_LIMIT
        ),
        name="mgrit",
    )(sources, starts, coupling.reshape(1, RL), classes.T, inverses, coarse_rate)


def solution(mesh):
    in_specs = (
        P("tm", None, "space", None),
        P("tm", "space", None),
        P("space"),
        P("space", None),
        P(),
        P(),
    )
    cfg = (mesh.shape["tm"], mesh.shape["space"])
    body = functools.partial(shards, cfg)
    return jax.shard_map(
        body, mesh=mesh, in_specs=in_specs, out_specs=P("tm", None, "space", None), check_vma=False
    )
```

time: 194 us -> 30.2 us (0.16); the launches traced: 190 us -> 30.1 us
  waiting for transfers between devices: 107 us -> 0 us
  starting transfers between devices: 58.4 us -> 0 us
  Pallas kernels: 0 us -> 27.8 us
  matrix products: 11 us -> 0 us
  other arithmetic: 6.1 us -> 0 us
  local copies, waits for them, and re-layouts: 7.04 us -> 2.27 us
    ppermute x30 -> x0, waiting for transfers between devices: 107 us -> none  [the longest x8 51.3 us: passed_along(): return lax.ppermute(block, axis, route)]
    ppermute x30 -> x0, starting transfers between devices: 58.4 us -> none  [the longest x11 26.9 us: with_halo(): before = lax.ppermute(last, axis, up)]
    pallas_call x0 -> x1, Pallas kernels: none -> 27.8 us  [shards(): pl.pallas_call(functools.partial(kernel, cfg), out_shape=jax.ShapeDtypeSt...]
    dot_general x11 -> x0, matrix products: 11 us -> none  [advance(): jnp.einsum('krbj,cij->ckrbi', blocked, inverses, precision=lax.Precision....]
    add x21 -> x0, other arithmetic: 4.77 us -> none  [the longest x11 3 us: advance(): field + coupling[None, :, None] * (padded[:, :-2] + padded[:, 2:]) + source]
    slice x23 -> x0, local copies, waits for them, and re-layouts: 4.39 us -> none  [the longest x10 1.95 us: with_halo(): last = lax.slice_in_dim(x, length - width, length, axis=dim)]
  transfers between devices with their start and end apart: 30 -> 0, of which waited for: 29 -> 0; matrix products, arithmetic and copies ran while one was open for 1% -> 0% of each run, Pallas kernels for 0% -> 0%
where the time goes in v1:
time: 30.2 us; the launch traced here: 30.1 us
  Pallas kernels  27.8 us (92%)
  local copies, waits for them, and re-layouts  2.27 us (8%)
    pallas_call x1, Pallas kernels, shards(): pl.pallas_call(functools.partial(kernel, cfg), out_shape=jax.ShapeDtypeSt...  27.8 us
    unnamed x1, local copies, waits for them, and re-layouts  2.27 us

profile of v1, /device:TPU:30, one launch (start us, length us, event | category | flops | bytes accessed | tf_op | source)
XLA Modules:
  0.0 30.1 jit_solution(2111861134894523599)
XLA Ops:
  0.0 27.8 %mgrit.1 = f32[2,4,128,256]{3,2,1,0:T(8,128)} custom-call(f32[2,4,128,256]{3,2,1,0:T(8,128)} %sources.1, f32[2,128,256]{2,1,0:T(8,128)} %starts.1, f32[1,128]{1,0:T(1,128)} %bitcast.3, s32[2,128]{1,0:T(2,128)} %bitcast.2, f32[4,128,128]{2,1,0:T(8,128)} %inverses.1, f32[4,128]{1,0:T(4,128)} %rate.1), custom_call_target="tpu_custom_call" | custom-call | tf_op jit(solution)/shard_map/mgrit/pallas_call | solution.py:341
  27.8 2.3 %copy.8 = f32[2,4,128,256]{3,2,1,0:T(8,128)} copy(f32[2,4,128,256]{3,2,1,0:T(8,128)} %mgrit.1) | data formatting | bytes 2097152

commit v2 on v1

--- a/solution.py
+++ b/solution.py
@@ -8,8 +8,8 @@
 from jax.sharding import PartitionSpec as P
 
 PAD = 8
-CHUNKS = 3
-VMEM_LIMIT = 60 * 1024 * 1024
+CHUNKS = 9
+VMEM_LIMIT = 16 * 1024 * 1024
 MESH = pl.DeviceIdType.MESH
 
 
@@ -17,13 +17,13 @@
     return -(-x // 8) * 8
 
 
-def kernel(cfg, sources, starts, coupling, classes, inverses, rate, out,
-           F, S, CPH, CLH, CP, MK, OD, W, FIN, ENDS, RES, DEC, R, RP, EI, EP, EN, FW, DL, OB,
-           in_sem, hs, hr, es, er, rs, rr, fs, fr, ps, pr, out_sem):
+def kernel(cfg, sources, starts, coupling_in, classes_in, inverses_in, rate_in, out,
+           coupling, classes, inverses, rate, F, S, CPH, CLH, CP, MK, OD, W, FIN, ENDS, RES, DEC, R, RP, EI, EP, EN, FW, DL,
+           in_sem, hs, hr, es, er, rs, rr, fs, fr, ps, pr):
     tm, space = cfg
     G, RL, L = starts.shape
     steps = sources.shape[1]
-    C, LB, _ = inverses.shape
+    C, LB, _ = inverses_in.shape
     B = L // LB
     KH = C // 2
     T = 3 * steps - 1
@@ -41,6 +41,14 @@
     has_prev, has_next = t > 0, t < tm - 1
     has_pz, has_nz = t > 1, t < tm - 2
 
+    small = [
+        pltpu.make_async_copy(a, b, in_sem.at[1 + steps + i])
+        for i, (a, b) in enumerate(
+            [(inverses_in, inverses), (coupling_in, coupling), (classes_in, classes), (rate_in, rate)]
+        )
+    ]
+    for c in small:
+        c.start()
     own = pl.ds(HM, RL)
     in_starts = pltpu.make_async_copy(starts, F.at[:, pl.ds(PAD + HM, RL), :], in_sem.at[0])
     in_starts.start()
@@ -70,17 +78,21 @@
 
     down, up = [], []
     halves = [HM if T - (m + 1) > HM - 8 else ceil8(T - (m + 1)) for m in range(steps)]
-    down.append((coupling, CPH.at[0]))
-    up.append((coupling, CPH.at[1]))
-    down.append((classes, CLH.at[0]))
-    up.append((classes, CLH.at[1]))
-    down.append((starts.at[:, pl.ds(RL - HM, HM), :], F.at[:, pl.ds(PAD, HM), :]))
-    up.append((starts.at[:, pl.ds(0, HM), :], F.at[:, pl.ds(PAD + HM + RL, HM), :]))
-    for m in range(steps):
-        h = halves[m]
-        down.append((sources.at[:, m, pl.ds(RL - h, h), :], S.at[:, m, pl.ds(HM - h, h), :]))
-        up.append((sources.at[:, m, pl.ds(0, h), :], S.at[:, m, pl.ds(HM + RL, h), :]))
-    n_halo = len(down)
+    down.append((coupling_in, CPH.at[0]))
+    up.append((coupling_in, CPH.at[1]))
+    down.append((classes_in, CLH.at[0]))
+    up.append((classes_in, CLH.at[1]))
+    order = [G - 1] + list(range(G - 1))
+    needs = {}
+    for g in order:
+        needs[g, 0] = [len(down)]
+        down.append((starts.at[g, pl.ds(RL - HM, HM), :], F.at[g, pl.ds(PAD, HM), :]))
+        up.append((starts.at[g, pl.ds(0, HM), :], F.at[g, pl.ds(PAD + HM + RL, HM), :]))
+        for m in range(steps):
+            h = halves[m]
+            needs.setdefault((g, m), []).append(len(down))
+            down.append((sources.at[g, m, pl.ds(RL - h, h), :], S.at[g, m, pl.ds(HM - h, h), :]))
+            up.append((sources.at[g, m, pl.ds(0, h), :], S.at[g, m, pl.ds(HM + RL, h), :]))
     down = [remote(a, b, hs.at[0, i], hr.at[0, i], (t, s + 1)) for i, (a, b) in enumerate(down)]
     up = [remote(a, b, hs.at[1, i], hr.at[1, i], (t, s - 1)) for i, (a, b) in enumerate(up)]
 
@@ -111,6 +123,9 @@
     for g in range(G):
         F[g, pl.ds(0, PAD), :] = jnp.zeros((PAD, L), f32)
         F[g, pl.ds(PAD + HM * 2 + RL, PAD), :] = jnp.zeros((PAD, L), f32)
+
+    for c in small:
+        c.wait()
 
     for k in range(KH):
         for o in range(2):
@@ -142,16 +157,18 @@
     CP[own, :] = column(coupling[...])
     fields(HM, classes[...], slice(0, RL), RL)
 
-    @pl.when(has_up)
-    def _():
-        for c in down:
-            c.wait_recv()
-
-    @pl.when(has_dn)
-    def _():
-        for c in up:
-            c.wait_recv()
-
+    def arrived(which):
+        @pl.when(has_up)
+        def _():
+            for i in which:
+                down[i].wait_recv()
+
+        @pl.when(has_dn)
+        def _():
+            for i in which:
+                up[i].wait_recv()
+
+    arrived([0, 1])
     CP[pl.ds(0, HM), :] = column(CPH[0])[RL - HM :]
     CP[pl.ds(HM + RL, HM), :] = column(CPH[1])[:HM]
     fields(0, CLH[0], slice(RL - HM, RL), HM)
@@ -163,10 +180,6 @@
 
     big = pl.ds(HM - HB, NB)
     fbig = pl.ds(PAD + HM - HB, NB)
-
-    @pl.when(jnp.logical_not(has_prev))
-    def _():
-        FIN[...] = F[0, fbig, :]
 
     def phi(g, m, t_step):
         h = ceil8(T - t_step)
@@ -191,14 +204,21 @@
             res.append(jnp.where(odd, yb[:, LB:], yb[:, :LB]))
         return jnp.concatenate(res, axis=1), lo, n
 
-    def relax(g, first):
+    def relax(g, first, fresh=False):
         for m in range(steps - 1):
+            if fresh:
+                arrived(needs[g, m])
+                if g == 0 and m == 0:
+                    @pl.when(jnp.logical_not(has_prev))
+                    def _():
+                        FIN[...] = F[0, fbig, :]
             res, lo, n = phi(g, m, first + m)
             F[g, pl.ds(PAD + lo, n), :] = res
 
     send_ends = remote(ENDS.at[G - 1], FIN, es.at[0], er.at[0], (t + 1, s))
-    for g in [G - 1] + list(range(G - 1)):
-        relax(g, 1)
+    for g in order:
+        relax(g, 1, True)
+        arrived(needs[g, steps - 1])
         res, lo, n = phi(g, steps - 1, steps)
         ENDS[g] = res
         if g == G - 1:
@@ -225,8 +245,13 @@
     R[...] = acc
     keep = pl.multiple_of((1 - p) * HALF, 8)
     give = pl.multiple_of(p * HALF, 8)
-    swap = remote(R.at[pl.ds(give, HALF), :], RP, rs.at[0], rr.at[0], (partner, s))
-    swap.start()
+    swap = [
+        remote(R.at[pl.ds(pl.multiple_of(give + j * CH, 8), CH), :], RP.at[pl.ds(j * CH, CH)],
+               rs.at[j], rr.at[j], (partner, s))
+        for j in range(CHUNKS)
+    ]
+    for c in swap:
+        c.start()
 
     @pl.when(jnp.logical_not(has_pz))
     def _():
@@ -236,8 +261,8 @@
     forward = [remote(FW.at[c], EI.at[c], fs.at[j], fr.at[j], (t + 2, s)) for j, c in enumerate(chunk)]
     deliver0 = [remote(DL.at[c], EP.at[c], ps.at[j], pr.at[j], (partner, s)) for j, c in enumerate(chunk)]
     deliver1 = [remote(EI.at[c], EP.at[c], ps.at[j], pr.at[j], (partner, s)) for j, c in enumerate(chunk)]
-    swap.wait_recv()
     for j in range(CHUNKS):
+        swap[j].wait_recv()
         mine = pl.ds(pl.multiple_of(keep + j * CH, 8), CH)
         c = chunk[j]
         d1 = DEC[pl.ds(pl.multiple_of(HM - HB + keep + j * CH, 8), CH), :]
@@ -275,29 +300,19 @@
     EN[pl.ds(give, HALF), :] = EP[...]
 
     e = EN[...]
-    outs = []
     F[0, fbig, :] = FIN[...] + e
     for g in range(G):
         e = dec * e + RES[g]
         fin = ENDS[g] + e
-        OB[g, steps - 1] = fin[HB : HB + RL]
+        out[g, steps - 1] = fin[HB : HB + RL]
         if g + 1 < G:
             F[g + 1, fbig, :] = fin
-    for g in range(G):
-        c = pltpu.make_async_copy(OB.at[g, steps - 1], out.at[g, steps - 1], out_sem.at[g, steps - 1])
-        c.start()
-        outs.append(c)
     for m in range(steps - 1):
         for g in range(G):
             res, lo, n = phi(g, m, 2 * steps + 1 + m)
             if m < steps - 2:
                 F[g, pl.ds(PAD + lo, n), :] = res
-            OB[g, m] = res[HM - lo : HM - lo + RL]
-            c = pltpu.make_async_copy(OB.at[g, m], out.at[g, m], out_sem.at[g, m])
-            c.start()
-            outs.append(c)
-    for c in outs:
-        c.wait()
+            out[g, m] = res[HM - lo : HM - lo + RL]
 
     @pl.when(has_dn)
     def _():
@@ -313,7 +328,8 @@
     def _():
         send_ends.wait_send()
 
-    swap.wait_send()
+    for c in swap:
+        c.wait_send()
 
     @pl.when(has_nz)
     def _():
@@ -337,13 +353,17 @@
     f32, bf16 = jnp.float32, jnp.bfloat16
     dma = pltpu.SemaphoreType.DMA
     vm = pltpu.VMEM
-    n_halo = 3 + steps
+    n_halo = 2 + G * (1 + steps)
     return pl.pallas_call(
         functools.partial(kernel, cfg),
         out_shape=jax.ShapeDtypeStruct(sources.shape, f32),
-        in_specs=[pl.BlockSpec(memory_space=pl.ANY)] * 2 + [pl.BlockSpec(memory_space=pltpu.VMEM)] * 4,
-        out_specs=pl.BlockSpec(memory_space=pl.ANY),
+        in_specs=[pl.BlockSpec(memory_space=pltpu.HBM)] * 6,
+        out_specs=pl.BlockSpec(memory_space=pltpu.VMEM),
         scratch_shapes=[
+            vm((1, RL), f32),
+            vm((B, RL), jnp.int32),
+            vm((C, LB, LB), f32),
+            vm((C, LB), f32),
             vm((G, E + 2 * PAD, L), f32),
             vm((G, steps, E, L), f32),
             vm((2, 1, RL), f32),
@@ -363,20 +383,21 @@
             vm((NB, L), f32),
             vm((HALF, L), f32),
             vm((HALF, L), f32),
-            vm((G, steps, RL, L), f32),
-            dma((1 + steps,)),
+            dma((5 + steps,)),
             dma((2, n_halo)), dma((2, n_halo)),
-            dma((1,)), dma((1,)),
             dma((1,)), dma((1,)),
             dma((CHUNKS,)), dma((CHUNKS,)),
             dma((CHUNKS,)), dma((CHUNKS,)),
-            dma((G, steps)),
+            dma((CHUNKS,)), dma((CHUNKS,)),
         ],
         compiler_params=pltpu.CompilerParams(
             collective_id=0, has_side_effects=True, vmem_limit_bytes=VMEM_LIMIT
         ),
         name="mgrit",
-    )(sources, starts, coupling.reshape(1, RL), classes.T, inverses, coarse_rate)
+    )(*[
+        pltpu.with_memory_space_constraint(a, pltpu.HBM)
+        for a in (sources, starts, coupling.reshape(1, RL), classes.T, inverses, coarse_rate)
+    ])
 
 
 def solution(mesh):

time: 30.2 us -> 26 us (0.86)
  Pallas kernels: 27.8 us -> 24.9 us
  local copies, waits for them, and re-layouts: 2.27 us -> 0.97 us
    pallas_call x1, Pallas kernels: 27.8 us -> 24.9 us  [shards(): pl.pallas_call(functools.partial(kernel, cfg), out_shape=jax.ShapeDtypeSt...]
    unnamed x1, local copies, waits for them, and re-layouts: 2.27 us -> 0.97 us
where the time goes in v2:
time: 26 us; the launch traced here: 25.9 us
  Pallas kernels  24.9 us (96%)
  local copies, waits for them, and re-layouts  0.97 us (4%)
    pallas_call x1, Pallas kernels, shards(): pl.pallas_call(functools.partial(kernel, cfg), out_shape=jax.ShapeDtypeSt...  24.9 us
    unnamed x1, local copies, waits for them, and re-layouts  0.97 us

profile of v2, /device:TPU:30, one launch (start us, length us, event | category | flops | bytes accessed | tf_op | source)
XLA Modules:
  0.0 25.9 jit_solution(9062041094480968086)
XLA Ops:
  0.0 24.9 %mgrit.1 = f32[2,4,128,256]{3,2,1,0:T(8,128)S(1)} custom-call(f32[2,4,128,256]{3,2,1,0:T(8,128)} %sources.1, f32[2,128,256]{2,1,0:T(8,128)} %starts.1, f32[1,128]{1,0:T(1,128)} %bitcast.3, s32[2,128]{1,0:T(2,128)} %bitcast.2, f32[4,128,128]{2,1,0:T(8,128)} %inverses_in.1, f32[4,128]{1,0:T(4,128)} %rate_in.1), custom_call_target="tpu_custom_call" | custom-call | tf_op jit(solution)/shard_map/mgrit/pallas_call | solution.py:357
  24.9 1.0 %copy.8 = f32[2,4,128,256]{3,2,1,0:T(8,128)} copy(f32[2,4,128,256]{3,2,1,0:T(8,128)S(1)} %mgrit.1) | data formatting | bytes 2097152

commit v3 on v2

--- a/solution.py
+++ b/solution.py
@@ -18,8 +18,8 @@
 
 
 def kernel(cfg, sources, starts, coupling_in, classes_in, inverses_in, rate_in, out,
-           coupling, classes, inverses, rate, F, S, CPH, CLH, CP, MK, OD, W, FIN, ENDS, RES, DEC, R, RP, EI, EP, EN, FW, DL,
-           in_sem, hs, hr, es, er, rs, rr, fs, fr, ps, pr):
+           coupling, classes, inverses, rate, F, S, CPH, CLH, CP, MK, OD, W, FIN, ENDS, RES, DEC, R, RP, RPB, QI, EI, EZ, EP, EN, FW, FW2, DL,
+           in_sem, hs, hr, es, er, rs, rr, qs, qr, fs, fr, ps, pr):
     tm, space = cfg
     G, RL, L = starts.shape
     steps = sources.shape[1]
@@ -39,7 +39,10 @@
     partner = t + 1 - 2 * p
     has_up, has_dn = s > 0, s < space - 1
     has_prev, has_next = t > 0, t < tm - 1
-    has_pz, has_nz = t > 1, t < tm - 2
+    has_pz, has_nz, has_nz2 = t > 1, t < tm - 2, t < tm - 4
+    odd = lax.rem(t // 2, 2) == 1
+    even = jnp.logical_not(odd)
+    left, right = p == 0, p == 1
 
     small = [
         pltpu.make_async_copy(a, b, in_sem.at[1 + steps + i])
@@ -64,6 +67,7 @@
         (has_up, (t, s - 1)), (has_dn, (t, s + 1)),
         (has_prev, (t - 1, s)), (has_next, (t + 1, s)),
         (has_pz, (t - 2, s)), (has_nz, (t + 2, s)),
+        (t > 3, (t - 4, s)), (has_nz2, (t + 4, s)),
     ]
     for cond, dev in peers:
         @pl.when(cond)
@@ -245,55 +249,112 @@
     R[...] = acc
     keep = pl.multiple_of((1 - p) * HALF, 8)
     give = pl.multiple_of(p * HALF, 8)
-    swap = [
-        remote(R.at[pl.ds(pl.multiple_of(give + j * CH, 8), CH), :], RP.at[pl.ds(j * CH, CH)],
-               rs.at[j], rr.at[j], (partner, s))
-        for j in range(CHUNKS)
-    ]
-    for c in swap:
-        c.start()
-
-    @pl.when(jnp.logical_not(has_pz))
-    def _():
-        EI[...] = jnp.zeros((HALF, L), f32)
-
     chunk = [pl.ds(j * CH, CH) for j in range(CHUNKS)]
-    forward = [remote(FW.at[c], EI.at[c], fs.at[j], fr.at[j], (t + 2, s)) for j, c in enumerate(chunk)]
-    deliver0 = [remote(DL.at[c], EP.at[c], ps.at[j], pr.at[j], (partner, s)) for j, c in enumerate(chunk)]
-    deliver1 = [remote(EI.at[c], EP.at[c], ps.at[j], pr.at[j], (partner, s)) for j, c in enumerate(chunk)]
-    for j in range(CHUNKS):
-        swap[j].wait_recv()
-        mine = pl.ds(pl.multiple_of(keep + j * CH, 8), CH)
-        c = chunk[j]
-        d1 = DEC[pl.ds(pl.multiple_of(HM - HB + keep + j * CH, 8), CH), :]
+
+    def rows(base, j):
+        return pl.ds(pl.multiple_of(base + j * CH, 8), CH)
+
+    def copies(src, dst, a, b, dev, base=0):
+        return [remote(src.at[rows(base, j)], dst.at[chunk[j]], a.at[j], b.at[j], dev)
+                for j in range(CHUNKS)]
+
+    def copies2(src, dst, a, b, dev, base, boff):
+        return [remote(src.at[rows(base, j)], dst.at[chunk[j]], a.at[CHUNKS + j], b.at[boff + j], dev)
+                for j in range(CHUNKS)]
+
+    swap = copies(R, RP, rs, rr, (partner, s), give)
+    swap2 = copies2(R, RPB, rs, rr, (partner, s), HALF, CHUNKS)
+    pass_a = copies(FW, QI, qs, qr, (t + 2, s))
+    pass_b = copies2(FW2, QI, qs, qr, (t + 1, s), 0, 0)
+    far = copies(FW, EI, fs, fr, (t + 4, s))
+    near = copies2(FW, EI, fs, fr, (t + 2, s), 0, 0)
+    deliver0 = copies(DL, EP, ps, pr, (partner, s))
+    deliver1 = copies(EZ, EP, ps, pr, (partner, s))
+
+    @pl.when(left & even)
+    def _():
+        for c in swap2:
+            c.start()
+
+    @pl.when(left | odd)
+    def _():
+        for c in swap:
+            c.start()
+
+    def power(base, j):
+        d1 = DEC[rows(base + HM - HB, j), :]
         D = d1
         for _ in range(1, G):
             D = D * d1
-        r_own, r_other = R[mine, :], RP[c, :]
-        first = jnp.where(p == 0, r_own, r_other)
-        second = jnp.where(p == 0, r_other, r_own)
-
-        @pl.when(has_pz)
-        def _():
-            forward[j].wait_recv()
-
-        mid = D * EI[c, :] + first
-
-        @pl.when(has_nz)
-        def _():
-            FW[c, :] = D * mid + second
-            forward[j].start()
-
-        @pl.when(p == 0)
-        def _():
-            DL[c, :] = mid
+        return D
+
+    @pl.when(right & even)
+    def _():
+        for j in range(CHUNKS):
+            swap2[j].wait_recv()
+
+            @pl.when(has_nz)
+            def _():
+                FW2[chunk[j], :] = power(HALF, j) * RPB[chunk[j], :] + R[rows(HALF, j), :]
+                pass_b[j].start()
+
+            swap[j].wait_recv()
+
+            @pl.when(has_nz)
+            def _():
+                FW[chunk[j], :] = power(0, j) * RP[chunk[j], :] + R[rows(0, j), :]
+                pass_a[j].start()
+
+    @pl.when(odd)
+    def _():
+        for j in range(CHUNKS):
+            swap[j].wait_recv()
+
+    @pl.when(jnp.where(odd, t < 4, t < 2))
+    def _():
+        EI[...] = jnp.zeros((HALF, L), f32)
+
+    for j in range(CHUNKS):
+        mine = rows(keep, j)
+        c = chunk[j]
+        D = power(keep, j)
+
+        @pl.when(jnp.where(odd, t > 3, t > 1))
+        def _():
+            far[j].wait_recv()
+
+        @pl.when(odd)
+        def _():
+            pass_a[j].wait_recv()
+            ez = D * (D * EI[c, :]) + QI[c, :]
+            EZ[c, :] = ez
+            r_own, r_other = R[mine, :], RP[c, :]
+
+            @pl.when(has_nz)
+            def _():
+                first = jnp.where(left, r_own, r_other)
+                second = jnp.where(left, r_other, r_own)
+                FW[c, :] = D * (D * ez + first) + second
+                near[j].start()
+
+            @pl.when(has_nz2)
+            def _():
+                far[j].start()
+
+        @pl.when(even)
+        def _():
+            EZ[c, :] = EI[c, :]
+
+        @pl.when(left)
+        def _():
+            DL[c, :] = D * EZ[c, :] + R[mine, :]
             deliver0[j].start()
-            EN[mine, :] = EI[c, :]
-
-        @pl.when(p == 1)
+            EN[mine, :] = EZ[c, :]
+
+        @pl.when(right)
         def _():
             deliver1[j].start()
-            EN[mine, :] = mid
+            EN[mine, :] = D * EZ[c, :] + RP[c, :]
 
     for j in range(CHUNKS):
         deliver0[j].wait_recv()
@@ -328,14 +389,17 @@
     def _():
         send_ends.wait_send()
 
-    for c in swap:
-        c.wait_send()
-
-    @pl.when(has_nz)
-    def _():
-        for c in forward:
-            c.wait_send()
-
+    def sent(cond, cs):
+        @pl.when(cond)
+        def _():
+            for c in cs:
+                c.wait_send()
+
+    sent(left & even, swap2)
+    sent(left | odd, swap)
+    sent(right & even & has_nz, pass_a + pass_b)
+    sent(odd & has_nz2, far)
+    sent(odd & has_nz, near)
     for c in deliver0:
         c.wait_send()
 
@@ -377,17 +441,15 @@
             vm((G, NB, L), f32),
             vm((E, L), f32),
             vm((NB, L), f32),
-            vm((HALF, L), f32),
-            vm((HALF, L), f32),
-            vm((HALF, L), f32),
+            *[vm((HALF, L), f32)] * 6,
             vm((NB, L), f32),
-            vm((HALF, L), f32),
-            vm((HALF, L), f32),
+            *[vm((HALF, L), f32)] * 3,
             dma((5 + steps,)),
             dma((2, n_halo)), dma((2, n_halo)),
             dma((1,)), dma((1,)),
-            dma((CHUNKS,)), dma((CHUNKS,)),
-            dma((CHUNKS,)), dma((CHUNKS,)),
+            dma((2 * CHUNKS,)), dma((2 * CHUNKS,)),
+            dma((2 * CHUNKS,)), dma((CHUNKS,)),
+            dma((2 * CHUNKS,)), dma((CHUNKS,)),
             dma((CHUNKS,)), dma((CHUNKS,)),
         ],
         compiler_params=pltpu.CompilerParams(

time: 26 us -> 26.8 us (1.031)
  Pallas kernels: 24.9 us -> 25.6 us
    pallas_call x1, Pallas kernels: 24.9 us -> 25.6 us  [shards(): pl.pallas_call(functools.partial(kernel, cfg), out_shape=jax.ShapeDtypeSt...]
where the time goes in v3:
time: 26.8 us; the launch traced here: 26.5 us
  Pallas kernels  25.6 us (96%)
  local copies, waits for them, and re-layouts  0.97 us (4%)
    pallas_call x1, Pallas kernels, shards(): pl.pallas_call(functools.partial(kernel, cfg), out_shape=jax.ShapeDtypeSt...  25.6 us
    unnamed x1, local copies, waits for them, and re-layouts  0.97 us

profile of v3, /device:TPU:30, one launch (start us, length us, event | category | flops | bytes accessed | tf_op | source)
XLA Modules:
  0.0 26.5 jit_solution(16231257340750914380)
XLA Ops:
  0.0 25.6 %mgrit.1 = f32[2,4,128,256]{3,2,1,0:T(8,128)S(1)} custom-call(f32[2,4,128,256]{3,2,1,0:T(8,128)} %sources.1, f32[2,128,256]{2,1,0:T(8,128)} %starts.1, f32[1,128]{1,0:T(1,128)} %bitcast.3, s32[2,128]{1,0:T(2,128)} %bitcast.2, f32[4,128,128]{2,1,0:T(8,128)} %inverses_in.1, f32[4,128]{1,0:T(4,128)} %rate_in.1), custom_call_target="tpu_custom_call" | custom-call | tf_op jit(solution)/shard_map/mgrit/pallas_call | solution.py:421
  25.6 1.0 %copy.8 = f32[2,4,128,256]{3,2,1,0:T(8,128)} copy(f32[2,4,128,256]{3,2,1,0:T(8,128)S(1)} %mgrit.1) | data formatting | bytes 2097152

commit v4 on v3

--- a/solution.py
+++ b/solution.py
@@ -18,7 +18,7 @@
 
 
 def kernel(cfg, sources, starts, coupling_in, classes_in, inverses_in, rate_in, out,
-           coupling, classes, inverses, rate, F, S, CPH, CLH, CP, MK, OD, W, FIN, ENDS, RES, DEC, R, RP, RPB, QI, EI, EZ, EP, EN, FW, FW2, DL,
+           coupling, classes, inverses, rate, F, S, CPH, CLH, CP, MK, OD, W, FIN, ENDS, RES, DEC, R, RP, QI, EI, EZ, EP, EN, FW, DL,
            in_sem, hs, hr, es, er, rs, rr, qs, qr, fs, fr, ps, pr):
     tm, space = cfg
     G, RL, L = starts.shape
@@ -258,28 +258,15 @@
         return [remote(src.at[rows(base, j)], dst.at[chunk[j]], a.at[j], b.at[j], dev)
                 for j in range(CHUNKS)]
 
-    def copies2(src, dst, a, b, dev, base, boff):
-        return [remote(src.at[rows(base, j)], dst.at[chunk[j]], a.at[CHUNKS + j], b.at[boff + j], dev)
-                for j in range(CHUNKS)]
-
     swap = copies(R, RP, rs, rr, (partner, s), give)
-    swap2 = copies2(R, RPB, rs, rr, (partner, s), HALF, CHUNKS)
     pass_a = copies(FW, QI, qs, qr, (t + 2, s))
-    pass_b = copies2(FW2, QI, qs, qr, (t + 1, s), 0, 0)
     far = copies(FW, EI, fs, fr, (t + 4, s))
-    near = copies2(FW, EI, fs, fr, (t + 2, s), 0, 0)
+    near = [remote(FW.at[c], EI.at[c], fs.at[CHUNKS + j], fr.at[j], (t + 2, s)) for j, c in enumerate(chunk)]
     deliver0 = copies(DL, EP, ps, pr, (partner, s))
     deliver1 = copies(EZ, EP, ps, pr, (partner, s))
 
-    @pl.when(left & even)
-    def _():
-        for c in swap2:
-            c.start()
-
-    @pl.when(left | odd)
-    def _():
-        for c in swap:
-            c.start()
+    for c in swap:
+        c.start()
 
     def power(base, j):
         d1 = DEC[rows(base + HM - HB, j), :]
@@ -288,27 +275,18 @@
             D = D * d1
         return D
 
-    @pl.when(right & even)
-    def _():
-        for j in range(CHUNKS):
-            swap2[j].wait_recv()
-
-            @pl.when(has_nz)
-            def _():
-                FW2[chunk[j], :] = power(HALF, j) * RPB[chunk[j], :] + R[rows(HALF, j), :]
-                pass_b[j].start()
-
-            swap[j].wait_recv()
-
-            @pl.when(has_nz)
-            def _():
-                FW[chunk[j], :] = power(0, j) * RP[chunk[j], :] + R[rows(0, j), :]
-                pass_a[j].start()
-
-    @pl.when(odd)
-    def _():
-        for j in range(CHUNKS):
-            swap[j].wait_recv()
+    def pair(j):
+        r_own, r_other = R[rows(keep, j), :], RP[chunk[j], :]
+        return jnp.where(left, r_own, r_other), jnp.where(left, r_other, r_own)
+
+    for j in range(CHUNKS):
+        swap[j].wait_recv()
+
+        @pl.when(even & has_nz)
+        def _():
+            first, second = pair(j)
+            FW[chunk[j], :] = power(keep, j) * first + second
+            pass_a[j].start()
 
     @pl.when(jnp.where(odd, t < 4, t < 2))
     def _():
@@ -328,18 +306,19 @@
             pass_a[j].wait_recv()
             ez = D * (D * EI[c, :]) + QI[c, :]
             EZ[c, :] = ez
-            r_own, r_other = R[mine, :], RP[c, :]
 
             @pl.when(has_nz)
             def _():
-                first = jnp.where(left, r_own, r_other)
-                second = jnp.where(left, r_other, r_own)
+                first, second = pair(j)
                 FW[c, :] = D * (D * ez + first) + second
-                near[j].start()
 
             @pl.when(has_nz2)
             def _():
                 far[j].start()
+
+            @pl.when(has_nz)
+            def _():
+                near[j].start()
 
         @pl.when(even)
         def _():
@@ -395,9 +374,9 @@
             for c in cs:
                 c.wait_send()
 
-    sent(left & even, swap2)
-    sent(left | odd, swap)
-    sent(right & even & has_nz, pass_a + pass_b)
+    for c in swap:
+        c.wait_send()
+    sent(even & has_nz, pass_a)
     sent(odd & has_nz2, far)
     sent(odd & has_nz, near)
     for c in deliver0:
@@ -441,14 +420,14 @@
             vm((G, NB, L), f32),
             vm((E, L), f32),
             vm((NB, L), f32),
-            *[vm((HALF, L), f32)] * 6,
+            *[vm((HALF, L), f32)] * 5,
             vm((NB, L), f32),
-            *[vm((HALF, L), f32)] * 3,
+            *[vm((HALF, L), f32)] * 2,
             dma((5 + steps,)),
             dma((2, n_halo)), dma((2, n_halo)),
             dma((1,)), dma((1,)),
-            dma((2 * CHUNKS,)), dma((2 * CHUNKS,)),
-            dma((2 * CHUNKS,)), dma((CHUNKS,)),
+            dma((CHUNKS,)), dma((CHUNKS,)),
+            dma((CHUNKS,)), dma((CHUNKS,)),
             dma((2 * CHUNKS,)), dma((CHUNKS,)),
             dma((CHUNKS,)), dma((CHUNKS,)),
         ],

time: 26.8 us -> 26.1 us (0.974)
  Pallas kernels: 25.6 us -> 24.8 us
    pallas_call x1, Pallas kernels: 25.6 us -> 24.8 us  [shards(): pl.pallas_call(functools.partial(kernel, cfg), out_shape=jax.ShapeDtypeSt...]
where the time goes in v4:
time: 26.1 us; the launch traced here: 25.8 us
  Pallas kernels  24.8 us (95%)
  local copies, waits for them, and re-layouts  0.97 us (4%)
    pallas_call x1, Pallas kernels, shards(): pl.pallas_call(functools.partial(kernel, cfg), out_shape=jax.ShapeDtypeSt...  24.8 us
    unnamed x1, local copies, waits for them, and re-layouts  0.97 us

profile of v4, /device:TPU:30, one launch (start us, length us, event | category | flops | bytes accessed | tf_op | source)
XLA Modules:
  0.0 25.8 jit_solution(583650949556509488)
XLA Ops:
  0.0 24.8 %mgrit.1 = f32[2,4,128,256]{3,2,1,0:T(8,128)S(1)} custom-call(f32[2,4,128,256]{3,2,1,0:T(8,128)} %sources.1, f32[2,128,256]{2,1,0:T(8,128)} %starts.1, f32[1,128]{1,0:T(1,128)} %bitcast.3, s32[2,128]{1,0:T(2,128)} %bitcast.2, f32[4,128,128]{2,1,0:T(8,128)} %inverses_in.1, f32[4,128]{1,0:T(4,128)} %rate_in.1), custom_call_target="tpu_custom_call" | custom-call | tf_op jit(solution)/shard_map/mgrit/pallas_call | solution.py:400
  24.8 1.0 %copy.8 = f32[2,4,128,256]{3,2,1,0:T(8,128)} copy(f32[2,4,128,256]{3,2,1,0:T(8,128)S(1)} %mgrit.1) | data formatting | bytes 2097152
